TPU v7x, 32 devices: a whole 2x2x4 slice. The times are simulated.
32 devices in a mesh: dp: 16 (over z, x, core), tensor: 2 (over y).
Axes of the slice: x: 2, y: 2, z: 4, core: 2. Of those that a mesh axis runs over, the one named last changes fastest.
Arguments:
- tokens: bfloat16 [16384, 1024], P(('dp', 'tensor')), may hold values from -6 to 6
- cotangent: bfloat16 [16384, 1024], P(('dp', 'tensor')), may hold values from -6 to 6
- lengths: int32 [16, 4], P('dp'), may hold values from 1 to 512, 1024 in all within a row
- w_in: bfloat16 [1024, 3, 1024], P('dp', None, 'tensor'), may hold values from -0.1875 to 0.1875
- w_out: bfloat16 [1024, 1024], P('tensor', 'dp'), may hold values from -0.1875 to 0.1875
- w_gate_up: bfloat16 [1024, 2, 4608], P('dp', None, 'tensor'), may hold values from -0.1875 to 0.1875
- w_down: bfloat16 [4608, 1024], P('tensor', 'dp'), may hold values from -0.1875 to 0.1875
- conv_weight: float32 [3, 1024], P(None, 'tensor'), may hold values from -3 to 3
- norm_gains: float32 [2, 1024], replicated, may hold values from 0.1 to 1.9
Outputs:
- block_out: bfloat16 [16384, 1024], P(('dp', 'tensor'))
- grad_tokens: bfloat16 [16384, 1024], P(('dp', 'tensor'))
- grad_w_in: float32 [1024, 3, 1024], P('dp', None, 'tensor')
- grad_w_out: float32 [1024, 1024], P('tensor', 'dp')
- grad_w_gate_up: float32 [1024, 2, 4608], P('dp', None, 'tensor')
- grad_w_down: float32 [4608, 1024], P('tensor', 'dp')
- grad_conv_weight: float32 [3, 1024], P(None, 'tensor')
- grad_norm_gains: float32 [2, 1024], replicated
Inputs may be any that keep to these rules, and one draw needn't show every extreme that they name: Each row of lengths sums to 1024, and its largest entry is exactly 512.
All inputs are finite; a program needn't handle non-finite values.
Results may differ from a plain program's by a relative error of at most 0.015.
Values may be sent and summed in bfloat16 or wider, within the bound.
A program may use at most 192 MiB of HBM per device.

v0:
```python
import jax
import jax.numpy as jnp
from jax import lax
from jax.sharding import PartitionSpec as P

epsilon = 1e-05


def positions(seq_lengths, row_count):
    starts = jnp.cumsum(seq_lengths) - seq_lengths
    row_index = jnp.arange(row_count, dtype=jnp.int32)
    begun_at = jnp.where(starts[None, :] <= row_index[:, None], starts[None, :], jnp.int32(0))
    return row_index - jnp.max(begun_at, axis=1)


def delayed(values, steps):
    return jnp.concatenate([jnp.zeros((steps, values.shape[1]), values.dtype), values[:-steps]], 0)


def advanced(values, steps):
    return jnp.concatenate([values[steps:], jnp.zeros((steps, values.shape[1]), values.dtype)], 0)


def body(tokens, cotangent, lengths, w_in, w_out, w_gate_up, w_down, conv_weight, norm_gains):
    model_width = tokens.shape[1]
    chan_count = w_in.shape[2]
    full_in, full_out, full_gu, full_down = (
        lax.all_gather(w_in, "dp", axis=0, tiled=True),
        lax.all_gather(w_out, "dp", axis=1, tiled=True),
        lax.all_gather(w_gate_up, "dp", axis=0, tiled=True),
        lax.all_gather(w_down, "dp", axis=1, tiled=True),
    )
    x_float = tokens.astype(jnp.float32)
    rms_first = lax.rsqrt(jnp.mean(x_float * x_float, axis=1, keepdims=True) + epsilon)
    normed_first = (x_float * rms_first * norm_gains[0]).astype(jnp.bfloat16)
    first_all = lax.all_gather(normed_first, "tensor", axis=0, tiled=True)
    row_count = first_all.shape[0]
    position = positions(lengths[0], row_count)
    first_keep = (position >= 1).astype(jnp.float32)[:, None]
    second_keep = (position >= 2).astype(jnp.float32)[:, None]
    projected = jnp.einsum("rd,dkc->krc", first_all, full_in, preferred_element_type=jnp.float32)
    proj_b = projected[0]
    proj_c = projected[1]
    proj_x = projected[2]
    gated_in = proj_b * proj_x
    conv_out = (
        conv_weight[0] * gated_in
        + conv_weight[1] * delayed(gated_in, 1) * first_keep
        + conv_weight[2] * delayed(gated_in, 2) * second_keep
    )
    mixer_in = (proj_c * conv_out).astype(jnp.bfloat16)
    residual_mid = x_float + lax.psum_scatter(
        jnp.dot(mixer_in, full_out, preferred_element_type=jnp.float32),
        "tensor",
        scatter_dimension=0,
        tiled=True,
    )
    rms_second = lax.rsqrt(jnp.mean(residual_mid * residual_mid, axis=1, keepdims=True) + epsilon)
    normed_second = (residual_mid * rms_second * norm_gains[1]).astype(jnp.bfloat16)
    second_all = lax.all_gather(normed_second, "tensor", axis=0, tiled=True)
    gate_up = jnp.einsum("rd,dkf->krf", second_all, full_gu, preferred_element_type=jnp.float32)
    gate_pre = gate_up[0]
    up_pre = gate_up[1]
    sig_gate = jax.nn.sigmoid(gate_pre)
    hidden_act = (gate_pre * sig_gate * up_pre).astype(jnp.bfloat16)
    block_out = (
        residual_mid
        + lax.psum_scatter(
            jnp.dot(hidden_act, full_down, preferred_element_type=jnp.float32).astype(jnp.bfloat16),
            "tensor",
            scatter_dimension=0,
            tiled=True,
        ).astype(jnp.float32)
    ).astype(jnp.bfloat16)
    back_in, back_out, back_gu, back_down = (
        lax.all_gather(w_in, "dp", axis=0, tiled=True),
        lax.all_gather(w_out, "dp", axis=1, tiled=True),
        lax.all_gather(w_gate_up, "dp", axis=0, tiled=True),
        lax.all_gather(w_down, "dp", axis=1, tiled=True),
    )
    cot_all = lax.all_gather(cotangent, "tensor", axis=0, tiled=True)
    grad_act = jnp.einsum("rd,fd->rf", cot_all, back_down, preferred_element_type=jnp.float32)
    grad_down = jnp.einsum("rf,rd->fd", hidden_act, cot_all, preferred_element_type=jnp.float32)
    grad_gate = (grad_act * up_pre * sig_gate * (1.0 + gate_pre * (1.0 - sig_gate))).astype(
        jnp.bfloat16
    )
    grad_up = (grad_act * gate_pre * sig_gate).astype(jnp.bfloat16)
    grad_hidden = jnp.stack([grad_gate, grad_up])
    grad_gu = jnp.einsum("rd,krf->dkf", second_all, grad_hidden, preferred_element_type=jnp.float32)
    grad_normed2 = lax.psum_scatter(
        jnp.einsum("krf,dkf->rd", grad_hidden, back_gu, preferred_element_type=jnp.float32),
        "tensor",
        scatter_dimension=0,
        tiled=True,
    )
    scaled_two = grad_normed2 * norm_gains[1]
    grad_mid = (
        cotangent.astype(jnp.float32)
        + rms_second * scaled_two
        - residual_mid
        * (rms_second * rms_second * rms_second)
        * jnp.mean(scaled_two * residual_mid, axis=1, keepdims=True)
    )
    gain_two = jnp.sum(grad_normed2 * residual_mid * rms_second, axis=0)
    grad_mid_b = grad_mid.astype(jnp.bfloat16)
    mid_all = lax.all_gather(grad_mid_b, "tensor", axis=0, tiled=True)
    grad_mixer_in = jnp.einsum("rd,cd->rc", mid_all, back_out, preferred_element_type=jnp.float32)
    grad_wout = jnp.einsum("rc,rd->cd", mixer_in, mid_all, preferred_element_type=jnp.float32)
    grad_conv_out = grad_mixer_in * proj_c
    grad_gated = (
        conv_weight[0] * grad_conv_out
        + conv_weight[1] * advanced(grad_conv_out * first_keep, 1)
        + conv_weight[2] * advanced(grad_conv_out * second_keep, 2)
    )
    grad_taps = jnp.stack(
        [
            jnp.sum(grad_conv_out * gated_in, axis=0),
            jnp.sum(grad_conv_out * first_keep * delayed(gated_in, 1), axis=0),
            jnp.sum(grad_conv_out * second_keep * delayed(gated_in, 2), axis=0),
        ]
    )
    grad_proj = jnp.stack(
        [grad_gated * proj_x, grad_mixer_in * conv_out, grad_gated * proj_b]
    ).astype(jnp.bfloat16)
    grad_win = jnp.einsum("rd,krc->dkc", first_all, grad_proj, preferred_element_type=jnp.float32)
    grad_normed1 = lax.psum_scatter(
        jnp.einsum("krc,dkc->rd", grad_proj, back_in, preferred_element_type=jnp.float32).astype(
            jnp.bfloat16
        ),
        "tensor",
        scatter_dimension=0,
        tiled=True,
    ).astype(jnp.float32)
    scaled_one = grad_normed1 * norm_gains[0]
    grad_tokens = (
        grad_mid
        + rms_first * scaled_one
        - x_float
        * (rms_first * rms_first * rms_first)
        * jnp.mean(scaled_one * x_float, axis=1, keepdims=True)
    ).astype(jnp.bfloat16)
    gain_one = jnp.sum(grad_normed1 * x_float * rms_first, axis=0)
    tensor_index = lax.axis_index("tensor")
    taps_wide = lax.dynamic_update_slice(
        jnp.zeros((grad_taps.shape[0], model_width), jnp.float32),
        grad_taps,
        (jnp.int32(0), tensor_index * chan_count),
    )
    gain_sums, taps_sums = lax.psum((jnp.stack([gain_one, gain_two]), taps_wide), ("dp", "tensor"))
    grad_conv = lax.dynamic_slice_in_dim(taps_sums, tensor_index * chan_count, chan_count, 1)
    shard_in, shard_out, shard_gu, shard_down = (
        lax.psum_scatter(
            grad_win.astype(jnp.bfloat16), "dp", scatter_dimension=0, tiled=True
        ).astype(jnp.float32),
        lax.psum_scatter(
            grad_wout.astype(jnp.bfloat16), "dp", scatter_dimension=1, tiled=True
        ).astype(jnp.float32),
        lax.psum_scatter(
            grad_gu.astype(jnp.bfloat16), "dp", scatter_dimension=0, tiled=True
        ).astype(jnp.float32),
        lax.psum_scatter(
            grad_down.astype(jnp.bfloat16), "dp", scatter_dimension=1, tiled=True
        ).astype(jnp.float32),
    )
    return (block_out, grad_tokens, shard_in, shard_out, shard_gu, shard_down, grad_conv, gain_sums)


def solution(mesh):
    return jax.shard_map(
        body,
        mesh=mesh,
        in_specs=(
            P(("dp", "tensor"), None),
            P(("dp", "tensor"), None),
            P("dp", None),
            P("dp", None, "tensor"),
            P("tensor", "dp"),
            P("dp", None, "tensor"),
            P("tensor", "dp"),
            P(None, "tensor"),
            P(),
        ),
        out_specs=(
            P(("dp", "tensor"), None),
            P(("dp", "tensor"), None),
            P("dp", None, "tensor"),
            P("tensor", "dp"),
            P("dp", None, "tensor"),
            P("tensor", "dp"),
            P(None, "tensor"),
            P(),
        ),
        check_vma=False,
    )
```

profile of v0, /device:TPU:0, one launch (start us, length us, event | category | flops | bytes accessed | tf_op | source)
XLA Modules:
  0.0 930.3 jit_solution(14761908806801854093)
XLA Ops:
  14.5 34.1 %all-gather.9.cloned.1.call-done = bf16[1024,1024]{1,0:T(8,128)(2,1)} async-done(((bf16[512,1024]{1,0:T(8,128)(2,1)}), bf16[1024,1024]{1,0:T(8,128)(2,1)}) %all-gather.9.cloned.1.call-update) | async-done | bytes 2097168 | tf_op jit(solution)/shard_map/all_gather | solution.py:36
  48.6 47.7 %all-gather.11.cloned.1.call-done = bf16[1024,3,512]{2,0,1:T(8,128)(2,1)} async-done(((bf16[64,3,512]{2,0,1:T(8,128)(2,1)}), bf16[1024,3,512]{2,0,1:T(8,128)(2,1)}) %all-gather.11.cloned.1.call-update) | async-done | bytes 3145744 | tf_op jit(solution)/shard_map/all_gather | solution.py:28
  96.4 5.9 convolution_bitcast_fusion.1
  107.4 27.3 %all-gather.13.cloned.1.call-done = bf16[512,1024]{0,1:T(8,128)(2,1)} async-done(((bf16[512,64]{0,1:T(8,128)(2,1)}), bf16[512,1024]{0,1:T(8,128)(2,1)}) %all-gather.13.cloned.1.call-update) | async-done | bytes 1048592 | tf_op jit(solution)/shard_map/all_gather | solution.py:29
  134.8 4.5 fusion.32
  139.3 53.5 %reduce-scatter.9.cloned.1.call-done = f32[512,1024]{1,0:T(8,128)} async-done(((f32[1024,1024]{1,0:T(8,128)}), f32[512,1024]{1,0:T(8,128)}) %reduce-scatter.9.cloned.1.call-update) | async-done | bytes 2097168 | tf_op jit(solution)/shard_map/reduce_scatter | solution.py:52
  199.9 30.6 %all-gather.15.cloned.1.call-done = bf16[1024,1024]{1,0:T(8,128)(2,1)} async-done(((bf16[512,1024]{1,0:T(8,128)(2,1)}), bf16[1024,1024]{1,0:T(8,128)(2,1)}) %all-gather.15.cloned.1.call-update) | async-done | bytes 2097168 | tf_op jit(solution)/shard_map/all_gather | solution.py:60
  230.5 83.7 %all-gather.17.cloned.1.call-done = bf16[1024,2,2304]{2,0,1:T(8,128)(2,1)} async-done(((bf16[64,2,2304]{2,0,1:T(8,128)(2,1)}), bf16[1024,2,2304]{2,0,1:T(8,128)(2,1)}) %all-gather.17.cloned.1.call-update) | async-done | bytes 9437200 | tf_op jit(solution)/shard_map/all_gather | solution.py:30
  314.2 16.7 %convolution_bitcast_fusion = f32[2,1024,2304]{2,1,0:T(8,128)} fusion(bf16[1024,2,2304]{2,0,1:T(8,128)(2,1)} %all-gather.17.cloned.1.call-done, bf16[1024,1024]{1,0:T(8,128)(2,1)} %all-gather.15.cloned.1.call-done), kind=kOutput, calls=%fused_computation | convolution fusion | flops 9663676416 | bytes 30408704 | tf_op jit(solution)/shard_map/rd,dkf->krf/dot_general | solution.py:61
  330.9 16.3 %all-gather.21.cloned.1.call-done = bf16[1024,1024]{1,0:T(8,128)(2,1)} async-done(((bf16[512,1024]{1,0:T(8,128)(2,1)}), bf16[1024,1024]{1,0:T(8,128)(2,1)}) %all-gather.21.cloned.1.call-update) | async-done | bytes 2097168 | tf_op jit(solution)/shard_map/all_gather | solution.py:81
  347.2 55.4 %all-gather.19.cloned.1.call-done = bf16[2304,1024]{0,1:T(8,128)(2,1)} async-done(((bf16[2304,64]{0,1:T(8,128)(2,1)}), bf16[2304,1024]{0,1:T(8,128)(2,1)}) %all-gather.19.cloned.1.call-update) | async-done | bytes 4718608 | tf_op jit(solution)/shard_map/all_gather | solution.py:31
  402.7 17.2 %fusion.2 = (bf16[1,1024,2304]{2,1,0:T(8,128)(2,1)S(1)}, bf16[1,1024,2304]{2,1,0:T(8,128)(2,1)}, bf16[1024,2304]{1,0:T(8,128)(2,1)}) fusion(f32[2,1024,2304]{2,1,0:T(8,128)} %convolution_bitcast_fusion, bf16[1024,1024]{1,0:T(8,128)(2,1)} %all-gather.21.cloned.1.call-done, bf16[2304,1024]{0,1:T(8,128)(2,1)} %all-gather.19.cloned.1.call-done), kind=kOutput, calls=%fused_computation.18 | convolution fusion | flops 4869586944 | bytes 39845888 | tf_op jit(solution)/shard_map/rd,fd->rf/dot_general | solution.py:82
  422.1 15.2 %fusion.4 = f32[1024,1024]{1,0:T(8,128)} fusion(bf16[1024,2,2304]{2,0,1:T(8,128)(2,1)} %all-gather.17.cloned.1.call-done, bf16[1,1024,2304]{2,1,0:T(8,128)(2,1)} %get-tuple-element.45, bf16[1,1024,2304]{2,1,0:T(8,128)(2,1)S(1)} %get-tuple-element.44), kind=kOutput, calls=%fused_computation.25 | convolution fusion | flops 9668395008 | bytes 23068672 | tf_op jit(solution)/shard_map/krf,dkf->rd/dot_general | solution.py:91
  437.6 9.3 %convolution_convert_fusion.3 = bf16[1024,1024]{1,0:T(8,128)(2,1)} fusion(bf16[1024,2304]{1,0:T(8,128)(2,1)} %get-tuple-element.46, bf16[2304,1024]{0,1:T(8,128)(2,1)} %all-gather.19.cloned.1.call-done), kind=kOutput, calls=%fused_computation.60 | convolution fusion | flops 4832886784 | bytes 11534336 | tf_op jit(solution)/shard_map/dot_general | solution.py:69
  447.0 43.4 %reduce-scatter.13.cloned.1.call-done = f32[512,1024]{1,0:T(8,128)} async-done(((f32[1024,1024]{1,0:T(8,128)}), f32[512,1024]{1,0:T(8,128)}) %reduce-scatter.13.cloned.1.call-update) | async-done | bytes 2097168 | tf_op jit(solution)/shard_map/reduce_scatter | solution.py:90
  490.4 2.8 multiply_reduce_fusion
  493.2 31.2 %reduce-scatter.11.cloned.1.call-done = bf16[512,1024]{1,0:T(8,128)(2,1)} async-done(((bf16[1024,1024]{1,0:T(8,128)(2,1)}), bf16[512,1024]{1,0:T(8,128)(2,1)}) %reduce-scatter.11.cloned.1.call-update) | async-done | bytes 1048592 | tf_op jit(solution)/shard_map/reduce_scatter | solution.py:68
  524.5 5.2 fusion.29
  529.8 9.4 %convolution_convert_fusion.1 = bf16[2304,1024]{0,1:T(8,128)(2,1)} fusion(bf16[1024,2304]{1,0:T(8,128)(2,1)} %get-tuple-element.46, bf16[1024,1024]{1,0:T(8,128)(2,1)} %all-gather.21.cloned.1.call-done), kind=kOutput, calls=%fused_computation.10 | convolution fusion | flops 4834197504 | bytes 11534336 | tf_op jit(solution)/shard_map/rf,rd->fd/dot_general | solution.py:83
  539.3 23.7 %all-gather.23.cloned.1.call-done = bf16[1024,1024]{1,0:T(8,128)(2,1)} async-done(((bf16[512,1024]{1,0:T(8,128)(2,1)}), bf16[1024,1024]{1,0:T(8,128)(2,1)}) %all-gather.23.cloned.1.call-update) | async-done | bytes 2097168 | tf_op jit(solution)/shard_map/all_gather | solution.py:106
  563.0 3.9 convolution_convert_fusion.4
  566.9 16.6 %convolution_convert_fusion = bf16[1024,2,2304]{2,0,1:T(8,128)(2,1)} fusion(bf16[1,1024,2304]{2,1,0:T(8,128)(2,1)} %get-tuple-element.45, bf16[1,1024,2304]{2,1,0:T(8,128)(2,1)} %copy-done.20, bf16[1024,1024]{1,0:T(8,128)(2,1)} %all-gather.15.cloned.1.call-done), kind=kOutput, calls=%fused_computation.8 | convolution fusion | flops 9687269376 | bytes 20971520 | tf_op jit(solution)/shard_map/rd,krf->dkf/dot_general | solution.py:89
  584.7 4.6 multiply_reduce_fusion.3
  594.3 4.7 bitcast_convert_fusion
  600.3 6.6 convolution_convert_fusion.2
  606.9 35.4 %reduce-scatter.23.cloned.1.call-done = bf16[2304,64]{0,1:T(8,128)(2,1)} async-done(((bf16[2304,1024]{0,1:T(8,128)(2,1)}), bf16[2304,64]{0,1:T(8,128)(2,1)}) %reduce-scatter.23.cloned.1.call-update) | async-done | bytes 294928 | tf_op jit(solution)/shard_map/reduce_scatter | solution.py:161
  644.1 59.1 %reduce-scatter.19.cloned.1.call-done = bf16[512,64]{0,1:T(8,128)(2,1)} async-done(((bf16[512,1024]{0,1:T(8,128)(2,1)}), bf16[512,64]{0,1:T(8,128)(2,1)}) %reduce-scatter.19.cloned.1.call-update) | async-done | bytes 65552 | tf_op jit(solution)/shard_map/reduce_scatter | solution.py:155
  704.7 112.7 %reduce-scatter.21.cloned.1.call-done = bf16[64,2,2304]{2,0,1:T(8,128)(2,1)} async-done(((bf16[1024,2,2304]{2,0,1:T(8,128)(2,1)}), bf16[64,2,2304]{2,0,1:T(8,128)(2,1)}) %reduce-scatter.21.cloned.1.call-update) | async-done | bytes 589840 | tf_op jit(solution)/shard_map/reduce_scatter | solution.py:158
  820.1 31.0 %reduce-scatter.15.cloned.1.call-done = bf16[512,1024]{1,0:T(8,128)(2,1)} async-done(((bf16[1024,1024]{1,0:T(8,128)(2,1)}), bf16[512,1024]{1,0:T(8,128)(2,1)}) %reduce-scatter.15.cloned.1.call-update) | async-done | bytes 1048592 | tf_op jit(solution)/shard_map/reduce_scatter | solution.py:126
  853.3 40.4 %all-reduce.4 = (f32[3,1024]{1,0:T(4,128)S(1)}, f32[2,1024]{1,0:T(2,128)}) all-reduce(f32[3,1024]{1,0:T(4,128)S(1)} %maximum_dynamic-update-slice_fusion, f32[2,1024]{1,0:T(2,128)S(1)} %pad_maximum_fusion.8), channel_id=1, replica_groups=mesh['dp'=16,'tensor'=2] {'dp','tensor'}, use_global_device_ids=true, to_apply=%region_17.18 | all-reduce | flops 5120 | bytes 40960 | tf_op jit(solution)/shard_map/psum | solution.py:149
  894.2 3.2 fusion.7
  897.4 24.2 %reduce-scatter.17.cloned.1.call-done = bf16[64,3,512]{2,0,1:T(8,128)(2,1)} async-done(((bf16[1024,3,512]{2,0,1:T(8,128)(2,1)}), bf16[64,3,512]{2,0,1:T(8,128)(2,1)}) %reduce-scatter.17.cloned.1.call-update) | async-done | bytes 196624 | tf_op jit(solution)/shard_map/reduce_scatter | solution.py:152
  (110 shorter events, 40.2 us)
Async XLA Ops:
  7.2 41.5 %all-gather.9.cloned.1.call-start = ((), (), s32[]{:S(2)}) async-start(), calls=%async_computation.8 | async-start | bytes 3145728 | tf_op jit(solution)/shard_map/all_gather | solution.py:36
  8.0 4.7 copy-start.12
  8.0 6.2 copy-start.19
  8.0 6.5 copy-start.17
  10.1 86.2 %copy-start.14 = (f32[512]{0:T(512)}, f32[512]{0:T(512)S(1)}, u32[]{:S(2)}) copy-start(f32[512]{0:T(512)S(1)} %get-tuple-element.59) | copy-start | bytes 6148
  12.7 83.7 %all-gather.11.cloned.1.call-start = ((), (), s32[]{:S(2)}) async-start(), calls=%async_computation.9 | async-start | bytes 3342336 | tf_op jit(solution)/shard_map/all_gather | solution.py:28
  13.4 121.3 %all-gather.13.cloned.1.call-start = ((), (), s32[]{:S(2)}) async-start(), calls=%async_computation.10 | async-start | bytes 1114112 | tf_op jit(solution)/shard_map/all_gather | solution.py:29
  14.2 178.6 %reduce-scatter.9.cloned.1.call-start = ((), (), s32[]{:S(2)}) async-start(), calls=%async_computation.11 | async-start | bytes 6291456 | tf_op jit(solution)/shard_map/reduce_scatter | solution.py:52
  102.3 2.6 copy-start
  107.4 31.8 %copy-start.6 = (bf16[1024,512]{1,0:T(8,128)(2,1)}, bf16[1024,512]{1,0:T(8,128)(2,1)S(1)}, u32[]{:S(2)}) copy-start(bf16[1024,512]{1,0:T(8,128)(2,1)S(1)} %get-tuple-element.42) | copy-start | bytes 3145732
  139.2 53.6 %copy-start.2 = (bf16[512,1024]{1,0:T(8,128)(2,1)S(1)}, bf16[512,1024]{1,0:T(8,128)(2,1)}, u32[]{:S(2)}) copy-start(bf16[512,1024]{1,0:T(8,128)(2,1)} %param.9) | copy-start | bytes 3145732
  139.2 91.3 %all-gather.15.cloned.1.call-start = ((), (), s32[]{:S(2)}) async-start(), calls=%async_computation.12 | async-start | bytes 3145728 | tf_op jit(solution)/shard_map/all_gather | solution.py:60
  197.2 116.9 %all-gather.17.cloned.1.call-start = ((), (), s32[]{:S(2)}) async-start(), calls=%async_computation.13 | async-start | bytes 10027008 | tf_op jit(solution)/shard_map/all_gather | solution.py:30
  198.2 149.0 %all-gather.21.cloned.1.call-start = ((), (), s32[]{:S(2)}) async-start(), calls=%async_computation.16 | async-start | bytes 3145728 | tf_op jit(solution)/shard_map/all_gather | solution.py:81
  199.0 203.7 %all-gather.19.cloned.1.call-start = ((), (), s32[]{:S(2)}) async-start(), calls=%async_computation.14 | async-start | bytes 5013504 | tf_op jit(solution)/shard_map/all_gather | solution.py:31
  199.7 290.7 %reduce-scatter.13.cloned.1.call-start = ((), (), s32[]{:S(2)}) async-start(), calls=%async_computation.17 | async-start | bytes 6291456 | tf_op jit(solution)/shard_map/reduce_scatter | solution.py:90
  437.3 87.1 %reduce-scatter.11.cloned.1.call-start = ((), (), s32[]{:S(2)}) async-start(), calls=%async_computation.15 | async-start | bytes 3145728 | tf_op jit(solution)/shard_map/reduce_scatter | solution.py:68
  447.0 77.5 %copy-start.4 = (bf16[512,1024]{1,0:T(8,128)(2,1)S(1)}, bf16[512,1024]{1,0:T(8,128)(2,1)}, u32[]{:S(2)}) copy-start(bf16[512,1024]{1,0:T(8,128)(2,1)} %param.10) | copy-start | bytes 3145732
  447.0 116.0 %all-gather.23.cloned.1.call-start = ((), (), s32[]{:S(2)}) async-start(), calls=%async_computation.18 | async-start | bytes 3145728 | tf_op jit(solution)/shard_map/all_gather | solution.py:106
  529.7 112.5 %reduce-scatter.23.cloned.1.call-start = ((), (), s32[]{:S(2)}) async-start(), calls=%async_computation.23 | async-start | bytes 5013504 | tf_op jit(solution)/shard_map/reduce_scatter | solution.py:161
  539.2 23.8 %copy-start.7 = (bf16[1024,512]{1,0:T(8,128)(2,1)S(1)}, bf16[1024,512]{1,0:T(8,128)(2,1)}, u32[]{:S(2)}) copy-start(bf16[1024,512]{1,0:T(8,128)(2,1)} %copy-done.6) | copy-start | bytes 3145732
  539.2 164.0 %reduce-scatter.19.cloned.1.call-start = ((), (), s32[]{:S(2)}) async-start(), calls=%async_computation.21 | async-start | bytes 1114112 | tf_op jit(solution)/shard_map/reduce_scatter | solution.py:155
  566.9 250.5 %reduce-scatter.21.cloned.1.call-start = ((), (), s32[]{:S(2)}) async-start(), calls=%async_computation.22 | async-start | bytes 10027008 | tf_op jit(solution)/shard_map/reduce_scatter | solution.py:158
  583.5 267.5 %reduce-scatter.15.cloned.1.call-start = ((), (), s32[]{:S(2)}) async-start(), calls=%async_computation.19 | async-start | bytes 3145728 | tf_op jit(solution)/shard_map/reduce_scatter | solution.py:126
  584.7 6.0 slice-start
  589.4 3.7 copy-start.9
  599.1 322.5 %reduce-scatter.17.cloned.1.call-start = ((), (), s32[]{:S(2)}) async-start(), calls=%async_computation.20 | async-start | bytes 3342336 | tf_op jit(solution)/shard_map/reduce_scatter | solution.py:152
  606.9 244.2 %copy-start.3 = (bf16[512,1024]{1,0:T(8,128)(2,1)S(1)}, bf16[512,1024]{1,0:T(8,128)(2,1)}, u32[]{:S(2)}) copy-start(bf16[512,1024]{1,0:T(8,128)(2,1)} %param.9) | copy-start | bytes 3145732
  606.9 244.2 %copy-start.13 = (f32[1,1024]{1,0:T(1,128)S(1)}, f32[1,1024]{1,0:T(1,128)}, u32[]{:S(2)}) copy-start(f32[1,1024]{1,0:T(1,128)} %copy-done.12) | copy-start | bytes 12292
  606.9 244.2 %copy-start.15 = (f32[512]{0:T(512)S(1)}, f32[512]{0:T(512)}, u32[]{:S(2)}) copy-start(f32[512]{0:T(512)} %copy-done.14) | copy-start | bytes 6148
  644.1 250.2 %copy-start.16 = (f32[512]{0:T(512)S(1)}, f32[512]{0:T(512)}, u32[]{:S(2)}) copy-start(f32[512]{0:T(512)} %get-tuple-element.58) | copy-start | bytes 6148
  851.1 43.2 %copy-start.5 = (bf16[512,1024]{1,0:T(8,128)(2,1)S(1)}, bf16[512,1024]{1,0:T(8,128)(2,1)}, u32[]{:S(2)}) copy-start(bf16[512,1024]{1,0:T(8,128)(2,1)} %reduce-scatter.15.cloned.1.call-done) | copy-start | bytes 3145732
  (7 other events, 11.2 us)
Sparse Core Ops, SparseCore 0:
  12.8 35.8 all-gather.8
  50.8 45.4 all-gather.10
  98.5 36.1 all-gather.12
  139.4 53.3 reduce-scatter.8
  197.4 33.0 all-gather.14
  233.2 80.9 all-gather.16
  315.7 31.4 all-gather.20
  349.5 53.1 all-gather.18
  437.5 52.9 reduce-scatter.12
  492.5 31.8 reduce-scatter.10
  529.8 33.0 all-gather.22
  566.7 75.5 reduce-scatter.22
  646.5 56.6 reduce-scatter.18
  707.1 110.2 reduce-scatter.20
  819.5 31.5 reduce-scatter.14
  854.7 66.8 reduce-scatter.16
where the time goes:
time: 936 us; the launch traced here: 930 us
  waiting for transfers between devices  712 us (76%)
  matrix products  115 us (12%)
  blocking collectives  40.4 us (4%)
  other arithmetic  31.9 us (3%)
  local copies, waits for them, and re-layouts  15.2 us (2%)
  between operations  14.7 us (2%)
    reduce_scatter x1, waiting for transfers between devices, body(): lax.psum_scatter(grad_gu.astype(jnp.bfloat16), 'dp', scatter_dimension=0,...  113 us
    all_gather x1, waiting for transfers between devices, body(): lax.all_gather(w_gate_up, 'dp', axis=0, tiled=True)  83.7 us
    reduce_scatter x1, waiting for transfers between devices, body(): lax.psum_scatter(grad_wout.astype(jnp.bfloat16), 'dp', scatter_dimension=...  59.1 us
    all_gather x1, waiting for transfers between devices, body(): lax.all_gather(w_down, 'dp', axis=1, tiled=True)  55.4 us
    reduce_scatter x1, waiting for transfers between devices, body(): lax.psum_scatter(jnp.dot(mixer_in, full_out, preferred_element_type=jnp.f...  53.5 us
    all_gather x1, waiting for transfers between devices, body(): lax.all_gather(w_in, 'dp', axis=0, tiled=True)  47.7 us
    reduce_scatter x1, waiting for transfers between devices, body(): lax.psum_scatter(jnp.einsum('krf,dkf->rd', grad_hidden, back_gu, preferre...  43.4 us
    psum x1, blocking collectives, body(): lax.psum((jnp.stack([gain_one, gain_two]), taps_wide), ('dp', 'tensor'))  40.4 us
  transfers between devices with their start and end apart: 16, of which 16 were waited for; matrix products, arithmetic and copies ran while one was open for 11% of the time, Pallas kernels for 0%

commit v1 on v0

v1 whole, which is shorter than its diff:
```python
import jax
import jax.numpy as jnp
from jax import lax
from jax.sharding import PartitionSpec as P

epsilon = 1e-05


def positions(seq_lengths, row_count):
    starts = jnp.cumsum(seq_lengths) - seq_lengths
    row_index = jnp.arange(row_count, dtype=jnp.int32)
    begun_at = jnp.where(starts[None, :] <= row_index[:, None], starts[None, :], jnp.int32(0))
    return row_index - jnp.max(begun_at, axis=1)


def delayed(values, steps):
    return jnp.concatenate([jnp.zeros((steps, values.shape[1]), values.dtype), values[:-steps]], 0)


def advanced(values, steps):
    return jnp.concatenate([values[steps:], jnp.zeros((steps, values.shape[1]), values.dtype)], 0)


def gather_rows(values):
    count = lax.axis_size("tensor")
    if count != 2:
        return lax.all_gather(values, "tensor", axis=0, tiled=True)
    rows = values.shape[0]
    index = lax.axis_index("tensor")
    other = lax.ppermute(values, "tensor", [(0, 1), (1, 0)])
    whole = jnp.zeros((2 * rows, values.shape[1]), values.dtype)
    whole = lax.dynamic_update_slice_in_dim(whole, values, index * rows, 0)
    return lax.dynamic_update_slice_in_dim(whole, other, (1 - index) * rows, 0)


def scatter_rows(values):
    count = lax.axis_size("tensor")
    if count != 2:
        return lax.psum_scatter(
            values.astype(jnp.bfloat16), "tensor", scatter_dimension=0, tiled=True
        ).astype(jnp.float32)
    rows = values.shape[0] // 2
    index = lax.axis_index("tensor")
    away = lax.dynamic_slice_in_dim(values, (1 - index) * rows, rows, 0).astype(jnp.bfloat16)
    other = lax.ppermute(away, "tensor", [(0, 1), (1, 0)])
    return lax.dynamic_slice_in_dim(values, index * rows, rows, 0) + other.astype(jnp.float32)


def butterfly_sum(values, axis):
    count = lax.axis_size(axis)
    if count & (count - 1):
        return lax.psum(values, axis)
    step = 1
    while step < count:
        values = values + lax.ppermute(values, axis, [(i, i ^ step) for i in range(count)])
        step *= 2
    return values


def body(tokens, cotangent, lengths, w_in, w_out, w_gate_up, w_down, conv_weight, norm_gains):
    shard_rows, taken, chan_count = w_in.shape
    hidden = w_gate_up.shape[2]
    packed = jnp.concatenate([w_in.reshape(shard_rows, taken * chan_count), w_out.T], axis=1)
    full_mix = lax.all_gather(packed, "dp", axis=0, tiled=True)
    full_gu = lax.all_gather(
        w_gate_up.reshape(shard_rows, 2 * hidden), "dp", axis=0, tiled=True
    )
    full_down = lax.all_gather(w_down.T, "dp", axis=0, tiled=True)
    full_in = full_mix[:, : taken * chan_count]
    full_out = full_mix[:, taken * chan_count :]
    x_float = tokens.astype(jnp.float32)
    rms_first = lax.rsqrt(jnp.mean(x_float * x_float, axis=1, keepdims=True) + epsilon)
    normed_first = (x_float * rms_first * norm_gains[0]).astype(jnp.bfloat16)
    first_all = gather_rows(normed_first)
    cot_all = gather_rows(cotangent)
    row_count = first_all.shape[0]
    position = positions(lengths[0], row_count)
    first_keep = (position >= 1).astype(jnp.float32)[:, None]
    second_keep = (position >= 2).astype(jnp.float32)[:, None]
    projected = jnp.dot(first_all, full_in, preferred_element_type=jnp.float32)
    proj_b = projected[:, :chan_count]
    proj_c = projected[:, chan_count : 2 * chan_count]
    proj_x = projected[:, 2 * chan_count :]
    gated_in = proj_b * proj_x
    conv_out = (
        conv_weight[0] * gated_in
        + conv_weight[1] * delayed(gated_in, 1) * first_keep
        + conv_weight[2] * delayed(gated_in, 2) * second_keep
    )
    mixer_in = (proj_c * conv_out).astype(jnp.bfloat16)
    residual_mid = x_float + scatter_rows(
        jnp.einsum("rc,dc->rd", mixer_in, full_out, preferred_element_type=jnp.float32)
    )
    rms_second = lax.rsqrt(jnp.mean(residual_mid * residual_mid, axis=1, keepdims=True) + epsilon)
    normed_second = (residual_mid * rms_second * norm_gains[1]).astype(jnp.bfloat16)
    second_all = gather_rows(normed_second)
    gate_up = jnp.dot(second_all, full_gu, preferred_element_type=jnp.float32)
    gate_pre = gate_up[:, :hidden]
    up_pre = gate_up[:, hidden:]
    sig_gate = jax.nn.sigmoid(gate_pre)
    hidden_act = (gate_pre * sig_gate * up_pre).astype(jnp.bfloat16)
    grad_down = jnp.einsum("rd,rf->df", cot_all, hidden_act, preferred_element_type=jnp.float32)
    sum_down = lax.psum_scatter(
        grad_down.astype(jnp.bfloat16), "dp", scatter_dimension=0, tiled=True
    )
    grad_act = jnp.einsum("rd,df->rf", cot_all, full_down, preferred_element_type=jnp.float32)
    grad_gate = (grad_act * up_pre * sig_gate * (1.0 + gate_pre * (1.0 - sig_gate))).astype(
        jnp.bfloat16
    )
    grad_up = (grad_act * gate_pre * sig_gate).astype(jnp.bfloat16)
    grad_hidden = jnp.concatenate([grad_gate, grad_up], axis=1)
    grad_gu = jnp.einsum("rd,rf->df", second_all, grad_hidden, preferred_element_type=jnp.float32)
    sum_gu = lax.psum_scatter(
        grad_gu.astype(jnp.bfloat16), "dp", scatter_dimension=0, tiled=True
    )
    grad_normed2 = scatter_rows(
        jnp.einsum("rf,df->rd", grad_hidden, full_gu, preferred_element_type=jnp.float32)
    )
    block_out = (
        residual_mid
        + scatter_rows(
            jnp.einsum("rf,df->rd", hidden_act, full_down, preferred_element_type=jnp.float32)
        )
    ).astype(jnp.bfloat16)
    scaled_two = grad_normed2 * norm_gains[1]
    grad_mid = (
        cotangent.astype(jnp.float32)
        + rms_second * scaled_two
        - residual_mid
        * (rms_second * rms_second * rms_second)
        * jnp.mean(scaled_two * residual_mid, axis=1, keepdims=True)
    )
    gain_two = jnp.sum(grad_normed2 * residual_mid * rms_second, axis=0)
    mid_all = gather_rows(grad_mid.astype(jnp.bfloat16))
    grad_mixer_in = jnp.dot(mid_all, full_out, preferred_element_type=jnp.float32)
    grad_wout = jnp.einsum("rd,rc->dc", mid_all, mixer_in, preferred_element_type=jnp.float32)
    grad_conv_out = grad_mixer_in * proj_c
    grad_gated = (
        conv_weight[0] * grad_conv_out
        + conv_weight[1] * advanced(grad_conv_out * first_keep, 1)
        + conv_weight[2] * advanced(grad_conv_out * second_keep, 2)
    )
    grad_taps = jnp.stack(
        [
            jnp.sum(grad_conv_out * gated_in, axis=0),
            jnp.sum(grad_conv_out * first_keep * delayed(gated_in, 1), axis=0),
            jnp.sum(grad_conv_out * second_keep * delayed(gated_in, 2), axis=0),
        ]
    )
    grad_proj = jnp.concatenate(
        [grad_gated * proj_x, grad_mixer_in * conv_out, grad_gated * proj_b], axis=1
    ).astype(jnp.bfloat16)
    grad_win = jnp.einsum("rd,rf->df", first_all, grad_proj, preferred_element_type=jnp.float32)
    sum_mix = lax.psum_scatter(
        jnp.concatenate([grad_win.astype(jnp.bfloat16), grad_wout.astype(jnp.bfloat16)], axis=1),
        "dp",
        scatter_dimension=0,
        tiled=True,
    )
    grad_normed1 = scatter_rows(
        jnp.einsum("rf,df->rd", grad_proj, full_in, preferred_element_type=jnp.float32)
    )
    scaled_one = grad_normed1 * norm_gains[0]
    grad_tokens = (
        grad_mid
        + rms_first * scaled_one
        - x_float
        * (rms_first * rms_first * rms_first)
        * jnp.mean(scaled_one * x_float, axis=1, keepdims=True)
    ).astype(jnp.bfloat16)
    gain_one = jnp.sum(grad_normed1 * x_float * rms_first, axis=0)
    model_width = tokens.shape[1]
    sums = butterfly_sum(
        jnp.concatenate([gain_one, gain_two, grad_taps.reshape(-1)]).reshape(-1, 128), "dp"
    ).reshape(-1)
    gain_sums = butterfly_sum(sums[: 2 * model_width].reshape(2, model_width), "tensor")
    grad_conv = sums[2 * model_width :].reshape(grad_taps.shape)
    split = taken * chan_count
    shard_in = sum_mix[:, :split].astype(jnp.float32).reshape(w_in.shape)
    shard_out = sum_mix[:, split:].astype(jnp.float32).T
    shard_gu = sum_gu.astype(jnp.float32).reshape(w_gate_up.shape)
    shard_down = sum_down.astype(jnp.float32).T
    return (block_out, grad_tokens, shard_in, shard_out, shard_gu, shard_down, grad_conv, gain_sums)


def solution(mesh):
    return jax.shard_map(
        body,
        mesh=mesh,
        in_specs=(
            P(("dp", "tensor"), None),
            P(("dp", "tensor"), None),
            P("dp", None),
            P("dp", None, "tensor"),
            P("tensor", "dp"),
            P("dp", None, "tensor"),
            P("tensor", "dp"),
            P(None, "tensor"),
            P(),
        ),
        out_specs=(
            P(("dp", "tensor"), None),
            P(("dp", "tensor"), None),
            P("dp", None, "tensor"),
            P("tensor", "dp"),
            P("dp", None, "tensor"),
            P("tensor", "dp"),
            P(None, "tensor"),
            P(),
        ),
        check_vma=False,
    )
```

time: 936 us -> 535 us (0.57)
  waiting for transfers between devices: 712 us -> 320 us
  blocking collectives: 40.4 us -> 0 us
  local copies, waits for them, and re-layouts: 15.2 us -> 39.8 us
  starting transfers between devices: 1.29 us -> 16.4 us
    all_gather x8 -> x3, waiting for transfers between devices: 319 us -> 53.2 us  [the longest x1 32.2 us: body(): full_down = lax.all_gather(w_down.T, 'dp', axis=0, tiled=True)]
    reduce_scatter x6 -> x1, waiting for transfers between devices: 242 us -> 0.01 us  [body(): lax.psum_scatter(jnp.concatenate([grad_win.astype(jnp.bfloat16), grad_wou...]
    ppermute x0 -> x13, waiting for transfers between devices: none -> 161 us  [the longest x4 76.1 us: scatter_rows(): other = lax.ppermute(away, 'tensor', [(0, 1), (1, 0)])]
    psum x1 -> x0, blocking collectives: 40.4 us -> none  [body(): lax.psum((jnp.stack([gain_one, gain_two]), taps_wide), ('dp', 'tensor'))]
    reduce_scatter x1, waiting for transfers between devices: 35.4 us -> 0.01 us  [body(): lax.psum_scatter(grad_down.astype(jnp.bfloat16), 'dp', scatter_dimension=...]
    ppermute x0 -> x13, starting transfers between devices: none -> 16.2 us  [the longest x4 6.48 us: gather_rows(): other = lax.ppermute(values, 'tensor', [(0, 1), (1, 0)])]
    convert_element_type x6 -> x0, other arithmetic: 14 us -> none  [the longest x1 5.22 us: body(): grad_mid_b = grad_mid.astype(jnp.bfloat16)]
    unnamed x48 -> x59, local copies, waits for them, and re-layouts: 13.3 us -> 18.8 us
  transfers between devices with their start and end apart: 16 -> 19, of which waited for: 16 -> 15; matrix products, arithmetic and copies ran while one was open for 11% -> 24% of each run, Pallas kernels for 0% -> 0%
where the time goes in v1:
time: 535 us; the launch traced here: 530 us
  waiting for transfers between devices  320 us (60%)
  matrix products  107 us (20%)
  local copies, waits for them, and re-layouts  39.8 us (7%)
  other arithmetic  31.2 us (6%)
  starting transfers between devices  16.4 us (3%)
  between operations  14.8 us (3%)
    reduce_scatter x1, waiting for transfers between devices, body(): lax.psum_scatter(grad_gu.astype(jnp.bfloat16), 'dp', scatter_dimension=0,...  106 us
    ppermute x4, waiting for transfers between devices, scatter_rows(): other = lax.ppermute(away, 'tensor', [(0, 1), (1, 0)])  76.1 us
    ppermute x4, waiting for transfers between devices, gather_rows(): other = lax.ppermute(values, 'tensor', [(0, 1), (1, 0)])  76 us
    all_gather x1, waiting for transfers between devices, body(): full_down = lax.all_gather(w_down.T, 'dp', axis=0, tiled=True)  32.2 us
    all_gather x1, waiting for transfers between devices, body(): full_mix = lax.all_gather(packed, 'dp', axis=0, tiled=True)  21 us
    unnamed x59, local copies, waits for them, and re-layouts  18.8 us
    dot_general x1, matrix products, body(): jnp.einsum('rd,df->rf', cot_all, full_down, preferred_element_type=jnp.fl...  18.4 us
    dot_general x1, matrix products, body(): gate_up = jnp.dot(second_all, full_gu, preferred_element_type=jnp.float32)  17 us
  transfers between devices with their start and end apart: 19, of which 15 were waited for; matrix products, arithmetic and copies ran while one was open for 24% of the time, Pallas kernels for 0%

profile of v1, /device:TPU:0, one launch (start us, length us, event | category | flops | bytes accessed | tf_op | source)
XLA Modules:
  0.0 529.8 jit_solution(8900568560652613607)
XLA Ops:
  15.0 3.0 collective-permute-start
  18.4 23.1 %collective-permute-done = bf16[512,1024]{0,1:T(8,128)(2,1)} collective-permute-done((bf16[512,1024]{0,1:T(8,128)(2,1)}, bf16[512,1024]{0,1:T(8,128)(2,1)}, u32[]{:S(2)}, u32[]{:S(2)}) %collective-permute-start) | collective-permute-done | bytes 1048608 | tf_op jit(solution)/shard_map/ppermute | solution.py:30
  42.9 21.0 %all-gather.4.cloned.1.call-done = bf16[1024,2048]{1,0:T(8,128)(2,1)} async-done(((bf16[64,2048]{1,0:T(8,128)(2,1)}), bf16[1024,2048]{1,0:T(8,128)(2,1)}) %all-gather.4.cloned.1.call-update) | async-done | bytes 4194320 | tf_op jit(solution)/shard_map/all_gather | solution.py:64
  63.8 5.5 %fusion.3 = f32[1024,1536]{1,0:T(8,128)S(1)} fusion(bf16[1024,1024]{0,1:T(8,128)(2,1)S(1)} %constant_dynamic-update-slice_fusion.6, bf16[1024,2048]{1,0:T(8,128)(2,1)} %all-gather.4.cloned.1.call-done), kind=kOutput, calls=%fused_computation.19 | convolution fusion | flops 3221225472 | bytes 11534336 | tf_op jit(solution)/shard_map/dot_general | solution.py:80
  71.9 3.1 multiply_convert_fusion.7
  75.0 2.9 fusion.16
  80.2 24.0 %collective-permute-done.1 = bf16[512,1024]{0,1:T(8,128)(2,1)S(1)} collective-permute-done((bf16[512,1024]{0,1:T(8,128)(2,1)S(1)}, bf16[512,1024]{0,1:T(8,128)(2,1)S(1)}, u32[]{:S(2)}, u32[]{:S(2)}) %collective-permute-start.1) | collective-permute-done | bytes 1048608 | tf_op jit(solution)/shard_map/ppermute | solution.py:45
  113.9 12.9 %collective-permute-done.4 = bf16[512,1024]{1,0:T(8,128)(2,1)} collective-permute-done((bf16[512,1024]{1,0:T(8,128)(2,1)}, bf16[512,1024]{1,0:T(8,128)(2,1)}, u32[]{:S(2)}, u32[]{:S(2)}) %collective-permute-start.4) | collective-permute-done | bytes 1048608 | tf_op jit(solution)/shard_map/ppermute | solution.py:30
  129.0 2.5 constant_dynamic-update-slice_fusion.2
  131.5 17.0 %collective-permute-done.2 = bf16[512,1024]{0,1:T(8,128)(2,1)} collective-permute-done((bf16[512,1024]{0,1:T(8,128)(2,1)}, bf16[512,1024]{0,1:T(8,128)(2,1)}, u32[]{:S(2)}, u32[]{:S(2)}) %collective-permute-start.2) | collective-permute-done | bytes 1048608 | tf_op jit(solution)/shard_map/ppermute | solution.py:30
  150.8 17.0 %fusion.26 = f32[1024,4608]{1,0:T(8,128)} fusion(bf16[1024,1024]{0,1:T(8,128)(2,1)} %constant_dynamic-update-slice_fusion.4, bf16[1024,4608]{1,0:T(8,128)(2,1)} %all-gather.6.cloned.1.call-done), kind=kOutput, calls=%fused_computation.94 | convolution fusion | flops 9663676416 | bytes 30408704 | tf_op jit(solution)/shard_map/dot_general | solution.py:97
  167.8 32.2 %all-gather.8.cloned.1.call-done = bf16[1024,2304]{1,0:T(8,128)(2,1)} async-done(((bf16[64,2304]{1,0:T(8,128)(2,1)}), bf16[1024,2304]{1,0:T(8,128)(2,1)}) %all-gather.8.cloned.1.call-update) | async-done | bytes 4718608 | tf_op jit(solution)/shard_map/all_gather | solution.py:68
  200.0 18.4 %multiply_convert_fusion.1 = (bf16[1024,2304]{1,0:T(8,128)(2,1)}, bf16[1024,2304]{1,0:T(8,128)(2,1)}, bf16[1024,2304]{1,0:T(8,128)(2,1)S(1)}) fusion(f32[1024,4608]{1,0:T(8,128)} %fusion.26, bf16[1024,1024]{0,1:T(8,128)(2,1)} %constant_dynamic-update-slice_fusion.2, bf16[1024,2304]{1,0:T(8,128)(2,1)} %all-gather.8.cloned.1.call-done), kind=kOutput, calls=%fused_computation.3 | convolution fusion | flops 4869586944 | bytes 39845888 | tf_op jit(solution)/shard_map/rd,df->rf/dot_general | solution.py:106
  220.5 8.9 %convolution_convert_fusion.1 = bf16[1024,2304]{1,0:T(8,128)(2,1)} fusion(bf16[1024,1024]{0,1:T(8,128)(2,1)} %constant_dynamic-update-slice_fusion.2, bf16[1024,2304]{1,0:T(8,128)(2,1)S(1)} %get-tuple-element.57), kind=kOutput, calls=%fused_computation.7 | convolution fusion | flops 4834197504 | bytes 11534336 | tf_op jit(solution)/shard_map/rd,rf->df/dot_general | solution.py:102
  229.4 8.3 %fusion.27 = f32[1024,1024]{0,1:T(8,128)S(1)} fusion(bf16[1024,2304]{1,0:T(8,128)(2,1)} %copy-done.24, bf16[1024,2304]{1,0:T(8,128)(2,1)} %all-gather.8.cloned.1.call-done), kind=kOutput, calls=%fused_computation.95 | convolution fusion | flops 4831838208 | bytes 13631488 | tf_op jit(solution)/shard_map/rf,df->rd/dot_general | solution.py:122
  242.4 16.0 %fusion = f32[1024,1024]{0,1:T(8,128)S(1)} fusion(bf16[1024,4608]{1,0:T(8,128)(2,1)} %all-gather.6.cloned.1.call-done, bf16[1024,2304]{1,0:T(8,128)(2,1)} %get-tuple-element.56, bf16[1024,2304]{1,0:T(8,128)(2,1)} %get-tuple-element.55), kind=kOutput, calls=%fused_computation.6 | convolution fusion | flops 9682550784 | bytes 23068672 | tf_op jit(solution)/shard_map/rf,df->rd/dot_general | solution.py:117
  259.0 8.2 %collective-permute-done.3 = bf16[512,1024]{0,1:T(8,128)(2,1)} collective-permute-done((bf16[512,1024]{0,1:T(8,128)(2,1)}, bf16[512,1024]{0,1:T(8,128)(2,1)}, u32[]{:S(2)}, u32[]{:S(2)}) %collective-permute-start.3) | collective-permute-done | bytes 1048608 | tf_op jit(solution)/shard_map/ppermute | solution.py:45
  267.2 21.6 %collective-permute-done.5 = bf16[512,1024]{0,1:T(8,128)(2,1)S(1)} collective-permute-done((bf16[512,1024]{0,1:T(8,128)(2,1)S(1)}, bf16[512,1024]{0,1:T(8,128)(2,1)S(1)}, u32[]{:S(2)}, u32[]{:S(2)}) %collective-permute-start.5) | collective-permute-done | bytes 1048608 | tf_op jit(solution)/shard_map/ppermute | solution.py:45
  288.8 3.2 multiply_reduce_fusion.3
  295.8 23.1 %collective-permute-done.6 = bf16[512,1024]{0,1:T(8,128)(2,1)S(1)} collective-permute-done((bf16[512,1024]{0,1:T(8,128)(2,1)S(1)}, bf16[512,1024]{0,1:T(8,128)(2,1)S(1)}, u32[]{:S(2)}, u32[]{:S(2)}) %collective-permute-start.6) | collective-permute-done | bytes 1048608 | tf_op jit(solution)/shard_map/ppermute | solution.py:30
  319.2 2.7 multiply_reduce_fusion.2
  327.2 3.9 convolution_convert_fusion.2
  331.1 2.6 pad_maximum_fusion.3
  333.8 16.8 %convolution_convert_fusion = bf16[1024,4608]{1,0:T(8,128)(2,1)} fusion(bf16[1024,1024]{0,1:T(8,128)(2,1)} %constant_dynamic-update-slice_fusion.4, bf16[1024,2304]{1,0:T(8,128)(2,1)} %get-tuple-element.56, bf16[1024,2304]{1,0:T(8,128)(2,1)} %get-tuple-element.55), kind=kOutput, calls=%fused_computation | convolution fusion | flops 9687269376 | bytes 20971520 | tf_op jit(solution)/shard_map/rd,rf->df/dot_general | solution.py:112
  350.6 5.5 %fusion.1 = f32[1024,1024]{0,1:T(8,128)S(1)} fusion(bf16[1024,2048]{1,0:T(8,128)(2,1)} %all-gather.4.cloned.1.call-done, bf16[1024,512]{1,0:T(8,128)(2,1)S(1)} %multiply_convert_fusion.3, bf16[1024,512]{1,0:T(8,128)(2,1)S(1)} %get-tuple-element.58, bf16[1024,512]{1,0:T(8,128)(2,1)S(1)} %get-tuple-element.42), kind=kOutput, calls=%fused_computation.17 | convolution fusion | flops 3230662656 | bytes 10485760 | tf_op jit(solution)/shard_map/rf,df->rd/dot_general | solution.py:161
  359.7 22.2 %collective-permute-done.7 = bf16[512,1024]{0,1:T(8,128)(2,1)S(1)} collective-permute-done((bf16[512,1024]{0,1:T(8,128)(2,1)S(1)}, bf16[512,1024]{0,1:T(8,128)(2,1)S(1)}, u32[]{:S(2)}, u32[]{:S(2)}) %collective-permute-start.7) | collective-permute-done | bytes 1048608 | tf_op jit(solution)/shard_map/ppermute | solution.py:45
  382.9 2.5 fusion.13
  387.3 3.2 collective-permute-done.9
  396.2 4.1 collective-permute-done.11
  401.9 3.6 fusion.10
  414.0 105.9 %reduce-scatter.6.cloned.1.call-done = bf16[64,4608]{1,0:T(8,128)(2,1)} async-done(((bf16[1024,4608]{1,0:T(8,128)(2,1)}), bf16[64,4608]{1,0:T(8,128)(2,1)}) %reduce-scatter.6.cloned.1.call-update) | async-done | bytes 589840 | tf_op jit(solution)/shard_map/reduce_scatter | solution.py:113
  519.9 2.8 reshape.120
  (143 shorter events, 67.3 us)
Async XLA Ops:
  7.2 4.7 copy-start.15
  7.2 56.7 %all-gather.4.cloned.1.call-start = ((), (), s32[]{:S(2)}) async-start(), calls=%async_computation.3 | async-start | bytes 4456448 | tf_op jit(solution)/shard_map/all_gather | solution.py:64
  9.8 141.0 %all-gather.6.cloned.1.call-start = ((), (), s32[]{:S(2)}) async-start(), calls=%async_computation.4 | async-start | bytes 10027008 | tf_op jit(solution)/shard_map/all_gather | solution.py:65
  11.8 188.2 %all-gather.8.cloned.1.call-start = ((), (), s32[]{:S(2)}) async-start(), calls=%async_computation.5 | async-start | bytes 5013504 | tf_op jit(solution)/shard_map/all_gather | solution.py:68
  12.5 91.7 %copy-start.1 = (bf16[512,1024]{0,1:T(8,128)(2,1)}, bf16[512,1024]{0,1:T(8,128)(2,1)S(1)}, u32[]{:S(2)}) copy-start(bf16[512,1024]{0,1:T(8,128)(2,1)S(1)} %copy.46) | copy-start | bytes 3145732
  15.0 26.5 %collective-permute-start = (bf16[512,1024]{0,1:T(8,128)(2,1)}, bf16[512,1024]{0,1:T(8,128)(2,1)}, u32[]{:S(2)}, u32[]{:S(2)}) collective-permute-start(bf16[512,1024]{0,1:T(8,128)(2,1)} %get-tuple-element.54), channel_id=1, source_target_pairs={{0,1},{1,0},{2,3},{3,2},{4,5},{5,4},{6,7},{7,6},{8,9},{9,8},{10,11... | collective-permute-start | bytes 3145736 | tf_op jit(solution)/shard_map/ppermute | solution.py:30
  18.0 390.9 %reduce-scatter.8.cloned.1.call-start = ((), (), s32[]{:S(2)}) async-start(), calls=%async_computation.8 | async-start | bytes 5013504 | tf_op jit(solution)/shard_map/reduce_scatter | solution.py:103
  42.9 21.0 %copy-start.13 = (bf16[1024,1024]{0,1:T(8,128)(2,1)}, bf16[1024,1024]{0,1:T(8,128)(2,1)S(1)}, u32[]{:S(2)}) copy-start(bf16[1024,1024]{0,1:T(8,128)(2,1)S(1)} %constant_dynamic-update-slice_fusion.6) | copy-start | bytes 6291460
  78.1 26.1 %collective-permute-start.1 = (bf16[512,1024]{0,1:T(8,128)(2,1)S(1)}, bf16[512,1024]{0,1:T(8,128)(2,1)S(1)}, u32[]{:S(2)}, u32[]{:S(2)}) collective-permute-start(bf16[512,1024]{0,1:T(8,128)(2,1)S(1)} %dynamic-slice_convert_fusion.3), channel_id=1, source_target_pairs={{0,1},{1,0},{2,3},{3,2},{4,5},{5,4},{6,7},{7,6},{8,9},{9,8},{10,11... | collective-permute-start | bytes 3145736 | tf_op jit(solution)/shard_map/ppermute | solution.py:45
  79.6 47.1 %collective-permute-start.4 = (bf16[512,1024]{1,0:T(8,128)(2,1)}, bf16[512,1024]{1,0:T(8,128)(2,1)}, u32[]{:S(2)}, u32[]{:S(2)}) collective-permute-start(bf16[512,1024]{1,0:T(8,128)(2,1)} %param.10), channel_id=1, source_target_pairs={{0,1},{1,0},{2,3},{3,2},{4,5},{5,4},{6,7},{7,6},{8,9},{9,8},{10,11... | collective-permute-start | bytes 3145736 | tf_op jit(solution)/shard_map/ppermute | solution.py:30
  108.2 40.3 %collective-permute-start.2 = (bf16[512,1024]{0,1:T(8,128)(2,1)}, bf16[512,1024]{0,1:T(8,128)(2,1)}, u32[]{:S(2)}, u32[]{:S(2)}) collective-permute-start(bf16[512,1024]{0,1:T(8,128)(2,1)} %get-tuple-element.48), channel_id=1, source_target_pairs={{0,1},{1,0},{2,3},{3,2},{4,5},{5,4},{6,7},{7,6},{8,9},{9,8},{10,11... | collective-permute-start | bytes 3145736 | tf_op jit(solution)/shard_map/ppermute | solution.py:30
  240.8 26.3 %collective-permute-start.3 = (bf16[512,1024]{0,1:T(8,128)(2,1)}, bf16[512,1024]{0,1:T(8,128)(2,1)}, u32[]{:S(2)}, u32[]{:S(2)}) collective-permute-start(bf16[512,1024]{0,1:T(8,128)(2,1)} %dynamic-slice_convert_fusion.2), channel_id=1, source_target_pairs={{0,1},{1,0},{2,3},{3,2},{4,5},{5,4},{6,7},{7,6},{8,9},{9,8},{10,11... | collective-permute-start | bytes 3145736 | tf_op jit(solution)/shard_map/ppermute | solution.py:45
  242.3 168.4 %reduce-scatter.4.cloned.1.call-start = ((), (), s32[]{:S(2)}) async-start(), calls=%async_computation.6 | async-start | bytes 4456448 | tf_op jit(solution)/shard_map/reduce_scatter | solution.py:154
  242.4 46.4 %copy-start.12 = (f32[1024,1024]{0,1:T(8,128)S(1)}, f32[1024,1024]{0,1:T(8,128)}, u32[]{:S(2)}) copy-start(f32[1024,1024]{0,1:T(8,128)} %copy-done.11) | copy-start | bytes 12582916
  258.4 30.4 %copy-start.4 = (f32[512,1024]{0,1:T(8,128)S(1)}, f32[512,1024]{0,1:T(8,128)}, u32[]{:S(2)}) copy-start(f32[512,1024]{0,1:T(8,128)} %copy-done.3) | copy-start | bytes 6291460
  258.6 30.2 %collective-permute-start.5 = (bf16[512,1024]{0,1:T(8,128)(2,1)S(1)}, bf16[512,1024]{0,1:T(8,128)(2,1)S(1)}, u32[]{:S(2)}, u32[]{:S(2)}) collective-permute-start(bf16[512,1024]{0,1:T(8,128)(2,1)S(1)} %dynamic-slice_convert_fusion.1), channel_id=1, source_target_pairs={{0,1},{1,0},{2,3},{3,2},{4,5},{5,4},{6,7},{7,6},{8,9},{9,8},{10,11... | collective-permute-start | bytes 3145736 | tf_op jit(solution)/shard_map/ppermute | solution.py:45
  292.0 27.1 %slice-start = ((s8[6291456]{0:T(1024)(128)(4,1)}), s8[4194304]{0:T(1024)(128)(4,1)S(1)}, s32[]{:S(2)}) async-start(s8[6291456]{0:T(1024)(128)(4,1)} %bitcast.52), calls=%async_computation.9 | async-start | bytes 8388608
  292.3 26.8 %slice-start.1 = ((s8[6291456]{0:T(1024)(128)(4,1)}), s8[2097152]{0:T(1024)(128)(4,1)S(1)}, s32[]{:S(2)}) async-start(s8[6291456]{0:T(1024)(128)(4,1)} %bitcast.52), calls=%async_computation.10 | async-start | bytes 4194304
  294.4 24.8 %copy-start.6 = (f32[1024,512]{1,0:T(8,128)S(1)}, f32[1024,512]{1,0:T(8,128)}, u32[]{:S(2)}) copy-start(f32[1024,512]{1,0:T(8,128)} %get-tuple-element.52) | copy-start | bytes 6291460
  294.4 24.6 %collective-permute-start.6 = (bf16[512,1024]{0,1:T(8,128)(2,1)S(1)}, bf16[512,1024]{0,1:T(8,128)(2,1)S(1)}, u32[]{:S(2)}, u32[]{:S(2)}) collective-permute-start(bf16[512,1024]{0,1:T(8,128)(2,1)S(1)} %get-tuple-element.45), channel_id=1, source_target_pairs={{0,1},{1,0},{2,3},{3,2},{4,5},{5,4},{6,7},{7,6},{8,9},{9,8},{10,11... | collective-permute-start | bytes 3145736 | tf_op jit(solution)/shard_map/ppermute | solution.py:30
  333.7 186.2 %reduce-scatter.6.cloned.1.call-start = ((), (), s32[]{:S(2)}) async-start(), calls=%async_computation.7 | async-start | bytes 10027008 | tf_op jit(solution)/shard_map/reduce_scatter | solution.py:113
  358.1 24.8 %copy-start.2 = (bf16[512,1024]{0,1:T(8,128)(2,1)S(1)}, bf16[512,1024]{0,1:T(8,128)(2,1)}, u32[]{:S(2)}) copy-start(bf16[512,1024]{0,1:T(8,128)(2,1)} %copy-done.1) | copy-start | bytes 3145732
  358.1 24.8 %copy-start.17 = (f32[1,1024]{1,0:T(1,128)S(1)}, f32[1,1024]{1,0:T(1,128)}, u32[]{:S(2)}) copy-start(f32[1,1024]{1,0:T(1,128)} %copy-done.16) | copy-start | bytes 12292
  358.1 24.8 %copy-start.19 = (f32[512]{0:T(512)S(1)}, f32[512]{0:T(512)}, u32[]{:S(2)}) copy-start(f32[512]{0:T(512)} %copy-done.18) | copy-start | bytes 6148
  358.2 23.7 %collective-permute-start.7 = (bf16[512,1024]{0,1:T(8,128)(2,1)S(1)}, bf16[512,1024]{0,1:T(8,128)(2,1)S(1)}, u32[]{:S(2)}, u32[]{:S(2)}) collective-permute-start(bf16[512,1024]{0,1:T(8,128)(2,1)S(1)} %dynamic-slice_convert_fusion), channel_id=1, source_target_pairs={{0,1},{1,0},{2,3},{3,2},{4,5},{5,4},{6,7},{7,6},{8,9},{9,8},{10,11... | collective-permute-start | bytes 3145736 | tf_op jit(solution)/shard_map/ppermute | solution.py:45
  385.5 16.4 %copy-start.5 = (f32[512,1024]{0,1:T(8,128)S(1)}, f32[512,1024]{0,1:T(8,128)}, u32[]{:S(2)}) copy-start(f32[512,1024]{0,1:T(8,128)} %get-tuple-element.46) | copy-start | bytes 6291460
  385.5 16.4 %copy-start.20 = (f32[512]{0:T(512)S(1)}, f32[512]{0:T(512)}, u32[]{:S(2)}) copy-start(f32[512]{0:T(512)} %get-tuple-element.69) | copy-start | bytes 6148
  385.5 1.2 collective-permute-start.8
  386.8 3.7 collective-permute-start.9
  390.5 4.4 collective-permute-start.10
  394.9 5.4 %collective-permute-start.11 = (f32[28,128]{1,0:T(8,128)S(1)}, f32[28,128]{1,0:T(8,128)S(1)}, u32[]{:S(2)}, u32[]{:S(2)}) collective-permute-start(f32[28,128]{1,0:T(8,128)S(1)} %add.133), channel_id=1, source_target_pairs={{0,16},{2,18},{4,20},{6,22},{8,24},{10,26},{12,28},{14,30},{16,0},... | collective-permute-start | bytes 43016 | tf_op jit(solution)/shard_map/ppermute | solution.py:55
  400.4 8.0 %collective-permute-start.12 = (f32[2,1024]{1,0:T(2,128)S(1)}, f32[2,1024]{1,0:T(2,128)S(1)}, u32[]{:S(2)}, u32[]{:S(2)}) collective-permute-start(f32[2,1024]{1,0:T(2,128)S(1)} %reshape.116), channel_id=1, source_target_pairs={{0,1},{1,0},{2,3},{3,2},{4,5},{5,4},{6,7},{7,6},{8,9},{9,8},{10,11... | collective-permute-start | bytes 24584 | tf_op jit(solution)/shard_map/ppermute | solution.py:55
  (14 other events, 32.8 us)
Sparse Core Ops, SparseCore 0:
  10.7 53.0 all-gather.3
  66.7 79.4 all-gather.5
  148.4 51.5 all-gather.7
  242.5 73.2 reduce-scatter.7
  333.8 71.4 reduce-scatter.3
  409.3 110.5 reduce-scatter.5

commit v2 on v1

--- a/solution.py
+++ b/solution.py
@@ -57,6 +57,41 @@
     return values
 
 
+def gather_blocks(shard, axis):
+    count = lax.axis_size(axis)
+    if count & (count - 1):
+        return lax.all_gather(shard, axis, axis=0, tiled=True)
+    index = lax.axis_index(axis)
+    blocks = shard[None]
+    step = count // 2
+    while step >= 1:
+        other = lax.ppermute(blocks, axis, [(i, i ^ step) for i in range(count)])
+        upper = (index // step) % 2 == 1
+        first = jnp.where(upper, other, blocks)
+        second = jnp.where(upper, blocks, other)
+        blocks = jnp.stack([first, second], axis=1).reshape((-1,) + shard.shape)
+        step //= 2
+    return blocks.reshape((-1,) + shard.shape[1:])
+
+
+def scatter_blocks(values, axis):
+    count = lax.axis_size(axis)
+    if count & (count - 1):
+        return lax.psum_scatter(values, axis, scatter_dimension=0, tiled=True)
+    index = lax.axis_index(axis)
+    shape = (values.shape[0] // count,) + values.shape[1:]
+    step = 1
+    while step < count:
+        pairs = values.reshape((count // step // 2, 2) + shape)
+        side = (index // step) % 2
+        away = lax.dynamic_index_in_dim(pairs, 1 - side, 1, keepdims=False)
+        kept = lax.dynamic_index_in_dim(pairs, side, 1, keepdims=False)
+        other = lax.ppermute(away, axis, [(i, i ^ step) for i in range(count)])
+        values = (kept.astype(jnp.float32) + other.astype(jnp.float32)).astype(values.dtype)
+        step *= 2
+    return values.reshape(shape)
+
+
 def body(tokens, cotangent, lengths, w_in, w_out, w_gate_up, w_down, conv_weight, norm_gains):
     shard_rows, taken, chan_count = w_in.shape
     hidden = w_gate_up.shape[2]
@@ -65,7 +100,7 @@
     full_gu = lax.all_gather(
         w_gate_up.reshape(shard_rows, 2 * hidden), "dp", axis=0, tiled=True
     )
-    full_down = lax.all_gather(w_down.T, "dp", axis=0, tiled=True)
+    full_down = gather_blocks(w_down.T, "dp")
     full_in = full_mix[:, : taken * chan_count]
     full_out = full_mix[:, taken * chan_count :]
     x_float = tokens.astype(jnp.float32)
@@ -100,9 +135,8 @@
     sig_gate = jax.nn.sigmoid(gate_pre)
     hidden_act = (gate_pre * sig_gate * up_pre).astype(jnp.bfloat16)
     grad_down = jnp.einsum("rd,rf->df", cot_all, hidden_act, preferred_element_type=jnp.float32)
-    sum_down = lax.psum_scatter(
-        grad_down.astype(jnp.bfloat16), "dp", scatter_dimension=0, tiled=True
-    )
+    grad_down, full_down = lax.optimization_barrier((grad_down.astype(jnp.bfloat16), full_down))
+    sum_down = lax.psum_scatter(grad_down, "dp", scatter_dimension=0, tiled=True)
     grad_act = jnp.einsum("rd,df->rf", cot_all, full_down, preferred_element_type=jnp.float32)
     grad_gate = (grad_act * up_pre * sig_gate * (1.0 + gate_pre * (1.0 - sig_gate))).astype(
         jnp.bfloat16
@@ -110,9 +144,12 @@
     grad_up = (grad_act * gate_pre * sig_gate).astype(jnp.bfloat16)
     grad_hidden = jnp.concatenate([grad_gate, grad_up], axis=1)
     grad_gu = jnp.einsum("rd,rf->df", second_all, grad_hidden, preferred_element_type=jnp.float32)
-    sum_gu = lax.psum_scatter(
-        grad_gu.astype(jnp.bfloat16), "dp", scatter_dimension=0, tiled=True
-    )
+    grad_gu, grad_gate, grad_up = lax.optimization_barrier(
+        (grad_gu.astype(jnp.bfloat16), grad_gate, grad_up)
+    )
+    grad_hidden = jnp.concatenate([grad_gate, grad_up], axis=1)
+    grad_gu, sum_down = lax.optimization_barrier((grad_gu, sum_down))
+    sum_gu = lax.psum_scatter(grad_gu, "dp", scatter_dimension=0, tiled=True)
     grad_normed2 = scatter_rows(
         jnp.einsum("rf,df->rd", grad_hidden, full_gu, preferred_element_type=jnp.float32)
     )
@@ -151,12 +188,10 @@
         [grad_gated * proj_x, grad_mixer_in * conv_out, grad_gated * proj_b], axis=1
     ).astype(jnp.bfloat16)
     grad_win = jnp.einsum("rd,rf->df", first_all, grad_proj, preferred_element_type=jnp.float32)
-    sum_mix = lax.psum_scatter(
-        jnp.concatenate([grad_win.astype(jnp.bfloat16), grad_wout.astype(jnp.bfloat16)], axis=1),
-        "dp",
-        scatter_dimension=0,
-        tiled=True,
-    )
+    grad_mix = jnp.concatenate(
+        [grad_win.astype(jnp.bfloat16), grad_wout.astype(jnp.bfloat16)], axis=1
+    )
+    sum_mix = scatter_blocks(grad_mix, "dp")
     grad_normed1 = scatter_rows(
         jnp.einsum("rf,df->rd", grad_proj, full_in, preferred_element_type=jnp.float32)
     )

time: 535 us -> 470 us (0.88)
  waiting for transfers between devices: 320 us -> 194 us
  local copies, waits for them, and re-layouts: 39.8 us -> 65 us
  starting transfers between devices: 16.4 us -> 39.2 us
  other arithmetic: 31.2 us -> 45.6 us
    reduce_scatter x3 -> x2, waiting for transfers between devices: 106 us -> 24 us  [the longest x1 24 us: body(): lax.psum_scatter(grad_down, 'dp', scatter_dimension=0, tiled=True)]
    ppermute x0 -> x8, waiting for transfers between devices: none -> 77.1 us  [the longest x4 65.7 us: gather_blocks(): other = lax.ppermute(blocks, axis, [(i, i ^ step) for i in range(count)])]
    ppermute x4, waiting for transfers between devices: 76 us -> 39 us  [gather_rows(): other = lax.ppermute(values, 'tensor', [(0, 1), (1, 0)])]
    all_gather x1 -> x0, waiting for transfers between devices: 32.2 us -> none  [body(): full_down = lax.all_gather(w_down.T, 'dp', axis=0, tiled=True)]
    ppermute x4, waiting for transfers between devices: 76.1 us -> 44.2 us  [scatter_rows(): other = lax.ppermute(away, 'tensor', [(0, 1), (1, 0)])]
    all_gather x1, waiting for transfers between devices: 21 us -> 0.01 us  [body(): full_mix = lax.all_gather(packed, 'dp', axis=0, tiled=True)]
    unnamed x59 -> x107, local copies, waits for them, and re-layouts: 18.8 us -> 33.4 us
    ppermute x0 -> x8, starting transfers between devices: none -> 11.8 us  [the longest x4 6.44 us: gather_blocks(): other = lax.ppermute(blocks, axis, [(i, i ^ step) for i in range(count)])]
  transfers between devices with their start and end apart: 19 -> 25, of which waited for: 15 -> 14; matrix products, arithmetic and copies ran while one was open for 24% -> 35% of each run, Pallas kernels for 0% -> 0%
where the time goes in v2:
time: 470 us; the launch traced here: 461 us
  waiting for transfers between devices  194 us (41%)
  matrix products  102 us (22%)
  local copies, waits for them, and re-layouts  65 us (14%)
  other arithmetic  45.6 us (10%)
  starting transfers between devices  39.2 us (8%)
  between operations  14.9 us (3%)
    ppermute x4, waiting for transfers between devices, gather_blocks(): other = lax.ppermute(blocks, axis, [(i, i ^ step) for i in range(count)])  65.7 us
    ppermute x4, waiting for transfers between devices, scatter_rows(): other = lax.ppermute(away, 'tensor', [(0, 1), (1, 0)])  44.2 us
    ppermute x4, waiting for transfers between devices, gather_rows(): other = lax.ppermute(values, 'tensor', [(0, 1), (1, 0)])  39 us
    unnamed x107, local copies, waits for them, and re-layouts  33.4 us
    reduce_scatter x1, waiting for transfers between devices, body(): lax.psum_scatter(grad_down, 'dp', scatter_dimension=0, tiled=True)  24 us
    dot_general x1, matrix products, body(): jnp.einsum('rd,df->rf', cot_all, full_down, preferred_element_type=jnp.fl...  16.8 us
    ppermute x5, starting transfers between devices, butterfly_sum(): lax.ppermute(values, axis, [(i, i ^ step) for i in range(count)])  16.4 us
    dot_general x1, matrix products, body(): jnp.einsum('rf,df->rd', grad_hidden, full_gu, preferred_element_type=jnp....  15.4 us
  transfers between devices with their start and end apart: 25, of which 14 were waited for; matrix products, arithmetic and copies ran while one was open for 35% of the time, Pallas kernels for 0%

profile of v2, /device:TPU:0, one launch (start us, length us, event | category | flops | bytes accessed | tf_op | source)
XLA Modules:
  0.0 460.6 jit_solution(4510045235525765596)
XLA Ops:
  11.9 4.1 collective-permute-start.4
  16.9 20.9 %collective-permute-done.4 = bf16[1,64,2304]{2,1,0:T(8,128)(2,1)S(1)} collective-permute-done((bf16[1,64,2304]{2,1,0:T(8,128)(2,1)S(1)}, bf16[1,64,2304]{2,1,0:T(8,128)(2,1)S(1)}, u32[]{:S(2)}, u32[]{:S(2)}) %collective-permute-start.4) | collective-permute-done | bytes 294944 | tf_op jit(solution)/shard_map/ppermute | solution.py:68
  44.1 21.5 %collective-permute-done.5 = bf16[2,64,2304]{2,1,0:T(8,128)(2,1)S(1)} collective-permute-done((bf16[2,64,2304]{2,1,0:T(8,128)(2,1)S(1)}, bf16[2,64,2304]{2,1,0:T(8,128)(2,1)S(1)}, u32[]{:S(2)}, u32[]{:S(2)}) %collective-permute-start.5) | collective-permute-done | bytes 589856 | tf_op jit(solution)/shard_map/ppermute | solution.py:68
  71.6 23.3 %collective-permute-done.6 = bf16[4,64,2304]{2,1,0:T(8,128)(2,1)S(1)} collective-permute-done((bf16[4,64,2304]{2,1,0:T(8,128)(2,1)S(1)}, bf16[4,64,2304]{2,1,0:T(8,128)(2,1)S(1)}, u32[]{:S(2)}, u32[]{:S(2)}) %collective-permute-start.6) | collective-permute-done | bytes 1179680 | tf_op jit(solution)/shard_map/ppermute | solution.py:68
  97.0 6.1 %fusion.10 = f32[1024,1536]{1,0:T(8,128)S(1)} fusion(bf16[1024,1024]{0,1:T(8,128)(2,1)} %constant_dynamic-update-slice_fusion.6, bf16[1024,2048]{1,0:T(8,128)(2,1)} %all-gather.3.cloned.1.call-done), kind=kOutput, calls=%fused_computation.27 | convolution fusion | flops 3221225472 | bytes 11534336 | tf_op jit(solution)/shard_map/dot_general | solution.py:115
  108.3 2.9 fusion.25
  125.4 14.7 %collective-permute-done.1 = bf16[512,1024]{0,1:T(8,128)(2,1)} collective-permute-done((bf16[512,1024]{0,1:T(8,128)(2,1)}, bf16[512,1024]{0,1:T(8,128)(2,1)}, u32[]{:S(2)}, u32[]{:S(2)}) %collective-permute-start.1) | collective-permute-done | bytes 1048608 | tf_op jit(solution)/shard_map/ppermute | solution.py:45
  152.8 17.6 %collective-permute-done.2 = bf16[512,1024]{0,1:T(8,128)(2,1)S(1)} collective-permute-done((bf16[512,1024]{0,1:T(8,128)(2,1)S(1)}, bf16[512,1024]{0,1:T(8,128)(2,1)S(1)}, u32[]{:S(2)}, u32[]{:S(2)}) %collective-permute-start.2) | collective-permute-done | bytes 1048608 | tf_op jit(solution)/shard_map/ppermute | solution.py:30
  171.6 14.1 %fusion.36 = f32[1024,4608]{1,0:T(8,128)S(1)} fusion(bf16[1024,1024]{0,1:T(8,128)(2,1)} %constant_dynamic-update-slice_fusion.4, bf16[1024,4608]{1,0:T(8,128)(2,1)} %all-gather.5.cloned.1.call-done), kind=kOutput, calls=%fused_computation.123 | convolution fusion | flops 9663676416 | bytes 30408704 | tf_op jit(solution)/shard_map/dot_general | solution.py:132
  185.7 3.2 multiply_convert_fusion.2
  189.0 3.7 copy-done.5
  194.8 6.7 %convolution_convert_fusion.1 = bf16[1024,2304]{1,0:T(8,128)(2,1)} fusion(bf16[1024,1024]{0,1:T(8,128)(2,1)S(1)} %copy-done.24, bf16[1024,2304]{1,0:T(8,128)(2,1)S(1)} %multiply_convert_fusion.2), kind=kOutput, calls=%fused_computation.12 | convolution fusion | flops 4834197504 | bytes 11534336 | tf_op jit(solution)/shard_map/rd,rf->df/dot_general | solution.py:137
  201.6 16.8 %multiply_convert_fusion.1 = (bf16[1024,2304]{1,0:T(8,128)(2,1)S(1)}, bf16[1024,2304]{1,0:T(8,128)(2,1)}) fusion(f32[1024,4608]{1,0:T(8,128)} %copy-done.5, bf16[1024,1024]{0,1:T(8,128)(2,1)} %constant_dynamic-update-slice_fusion.2, bf16[1024,2304]{1,0:T(8,128)(2,1)} %bitcast.116), kind=kOutput, calls=%fused_computation.9 | convolution fusion | flops 4862509056 | bytes 35127296 | tf_op jit(solution)/shard_map/rd,df->rf/dot_general | solution.py:140
  220.6 15.4 %convolution_convert_fusion = bf16[1024,4608]{1,0:T(8,128)(2,1)} fusion(bf16[1024,1024]{0,1:T(8,128)(2,1)} %constant_dynamic-update-slice_fusion.4, bf16[1024,2304]{1,0:T(8,128)(2,1)} %get-tuple-element.17, bf16[1024,2304]{1,0:T(8,128)(2,1)S(1)} %get-tuple-element.16), kind=kOutput, calls=%fused_computation | convolution fusion | flops 9687269376 | bytes 20971520 | tf_op jit(solution)/shard_map/rd,rf->df/dot_general | solution.py:146
  236.0 15.4 %fusion.3 = f32[1024,1024]{0,1:T(8,128)S(1)} fusion(bf16[1024,4608]{1,0:T(8,128)(2,1)} %all-gather.5.cloned.1.call-done, bf16[1024,2304]{1,0:T(8,128)(2,1)} %get-tuple-element.17, bf16[1024,2304]{1,0:T(8,128)(2,1)} %copy-done.46), kind=kOutput, calls=%fused_computation.4 | convolution fusion | flops 9682550784 | bytes 23068672 | tf_op jit(solution)/shard_map/rf,df->rd/dot_general | solution.py:154
  254.1 7.2 %fusion.37 = f32[1024,1024]{0,1:T(8,128)S(1)} fusion(bf16[1024,2304]{1,0:T(8,128)(2,1)} %copy-done.20, bf16[1024,2304]{1,0:T(8,128)(2,1)S(1)} %bitcast.119), kind=kOutput, calls=%fused_computation.124 | convolution fusion | flops 4831838208 | bytes 13631488 | tf_op jit(solution)/shard_map/rf,df->rd/dot_general | solution.py:159
  264.1 24.0 %reduce-scatter.3.cloned.1.call-done = bf16[64,2304]{1,0:T(8,128)(2,1)} async-done(((bf16[1024,2304]{1,0:T(8,128)(2,1)}), bf16[64,2304]{1,0:T(8,128)(2,1)}) %reduce-scatter.3.cloned.1.call-update) | async-done | bytes 294928 | tf_op jit(solution)/shard_map/reduce_scatter | solution.py:139
  288.2 11.0 %collective-permute-done.8 = bf16[512,1024]{0,1:T(8,128)(2,1)S(1)} collective-permute-done((bf16[512,1024]{0,1:T(8,128)(2,1)}, bf16[512,1024]{0,1:T(8,128)(2,1)S(1)}, u32[]{:S(2)}, u32[]{:S(2)}) %collective-permute-start.8) | collective-permute-done | bytes 1048608 | tf_op jit(solution)/shard_map/ppermute | solution.py:45
  299.2 5.9 %multiply_reduce_fusion.3 = (f32[1024]{0:T(1024)S(1)}, f32[512]{0:T(512)S(1)}, bf16[512,1024]{0,1:T(8,128)(2,1)}) fusion(f32[512,1024]{0,1:T(8,128)} %copy-done.3, f32[512]{0:T(512)S(1)} %get-tuple-element.101, bf16[512,1024]{0,1:T(8,128)(2,1)} %collective-permute-done.9, f32[1024,1024]{0,1:T(8,128)} %copy-done.16, s32[]{:T(128)S(6)} %select_n.142, ...), kind=kLoop, calls=%fused_computation.46 | loop fusion | flops 6289920 | bytes 9449476 | tf_op jit(solution)/shard_map/reduce_sum | solution.py:170
  307.0 3.4 constant_dynamic-update-slice_fusion.1
  313.2 21.4 %collective-permute-done.10 = bf16[512,1024]{0,1:T(8,128)(2,1)} collective-permute-done((bf16[512,1024]{0,1:T(8,128)(2,1)S(1)}, bf16[512,1024]{0,1:T(8,128)(2,1)}, u32[]{:S(2)}, u32[]{:S(2)}) %collective-permute-start.10) | collective-permute-done | bytes 1048608 | tf_op jit(solution)/shard_map/ppermute | solution.py:30
  336.9 4.2 multiply_reduce_fusion.2
  347.4 5.7 %convolution_convert_fusion.2 = bf16[1024,1536]{1,0:T(8,128)(2,1)S(1)} fusion(bf16[1024,1024]{0,1:T(8,128)(2,1)} %constant_dynamic-update-slice_fusion.6, bf16[1024,512]{1,0:T(8,128)(2,1)S(1)} %multiply_convert_fusion.3, bf16[1024,512]{1,0:T(8,128)(2,1)S(1)} %get-tuple-element.83, bf16[1024,512]{1,0:T(8,128)(2,1)S(1)} %get-tuple-element.64), kind=kOutput, calls=%fused_computation.23 | convolution fusion | flops 3232235520 | bytes 8388608 | tf_op jit(solution)/shard_map/rd,rf->df/dot_general | solution.py:190
  355.8 6.3 %fusion.8 = f32[1024,1024]{0,1:T(8,128)S(1)} fusion(bf16[1024,2048]{1,0:T(8,128)(2,1)} %all-gather.3.cloned.1.call-done, bf16[1024,512]{1,0:T(8,128)(2,1)} %copy-done.27, bf16[1024,512]{1,0:T(8,128)(2,1)} %copy-done.29, bf16[1024,512]{1,0:T(8,128)(2,1)S(1)} %get-tuple-element.64), kind=kOutput, calls=%fused_computation.25 | convolution fusion | flops 3230662656 | bytes 10485760 | tf_op jit(solution)/shard_map/rf,df->rd/dot_general | solution.py:196
  370.6 18.4 %collective-permute-done.11 = bf16[512,1024]{0,1:T(8,128)(2,1)} collective-permute-done((bf16[512,1024]{0,1:T(8,128)(2,1)}, bf16[512,1024]{0,1:T(8,128)(2,1)}, u32[]{:S(2)}, u32[]{:S(2)}) %collective-permute-start.11) | collective-permute-done | bytes 1048608 | tf_op jit(solution)/shard_map/ppermute | solution.py:45
  389.1 2.9 fusion.20
  392.0 8.8 %collective-permute-done.13 = bf16[4,64,2048]{2,1,0:T(8,128)(2,1)} collective-permute-done((bf16[4,64,2048]{2,1,0:T(8,128)(2,1)}, bf16[4,64,2048]{2,1,0:T(8,128)(2,1)}, u32[]{:S(2)}, u32[]{:S(2)}) %collective-permute-start.13) | collective-permute-done | bytes 1048608 | tf_op jit(solution)/shard_map/ppermute | solution.py:89
  412.5 5.9 %collective-permute-done.18 = f32[28,128]{1,0:T(8,128)S(1)} collective-permute-done((f32[28,128]{1,0:T(8,128)S(1)}, f32[28,128]{1,0:T(8,128)S(1)}, u32[]{:S(2)}, u32[]{:S(2)}) %collective-permute-start.18) | collective-permute-done | bytes 14368 | tf_op jit(solution)/shard_map/ppermute | solution.py:55
  418.4 11.7 %collective-permute-start.19 = (f32[28,128]{1,0:T(8,128)S(1)}, f32[28,128]{1,0:T(8,128)S(1)}, u32[]{:S(2)}, u32[]{:S(2)}) collective-permute-start(f32[28,128]{1,0:T(8,128)S(1)} %add.212), channel_id=1, source_target_pairs={{0,16},{2,18},{4,20},{6,22},{8,24},{10,26},{12,28},{14,30},{16,0},... | collective-permute-start | bytes 43016 | tf_op jit(solution)/shard_map/ppermute | solution.py:55
  434.8 3.0 collective-permute-start.15
  437.8 3.6 fusion.17
  450.8 2.8 reshape.164
  (221 shorter events, 113.1 us)
Async XLA Ops:
  7.2 89.8 %all-gather.3.cloned.1.call-start = ((), (), s32[]{:S(2)}) async-start(), calls=%async_computation.2 | async-start | bytes 4456448 | tf_op jit(solution)/shard_map/all_gather | solution.py:99
  9.9 161.7 %all-gather.5.cloned.1.call-start = ((), (), s32[]{:S(2)}) async-start(), calls=%async_computation.3 | async-start | bytes 10027008 | tf_op jit(solution)/shard_map/all_gather | solution.py:100
  11.9 276.3 %reduce-scatter.3.cloned.1.call-start = ((), (), s32[]{:S(2)}) async-start(), calls=%async_computation.4 | async-start | bytes 5013504 | tf_op jit(solution)/shard_map/reduce_scatter | solution.py:139
  11.9 25.9 %collective-permute-start.4 = (bf16[1,64,2304]{2,1,0:T(8,128)(2,1)S(1)}, bf16[1,64,2304]{2,1,0:T(8,128)(2,1)S(1)}, u32[]{:S(2)}, u32[]{:S(2)}) collective-permute-start(bf16[1,64,2304]{2,1,0:T(8,128)(2,1)S(1)} %bitcast.127), channel_id=1, source_target_pairs={{0,16},{2,18},{4,20},{6,22},{8,24},{10,26},{12,28},{14,30},{16,0},... | collective-permute-start | bytes 884744 | tf_op jit(solution)/shard_map/ppermute | solution.py:68
  16.6 123.5 %copy-start.1 = (bf16[512,1024]{0,1:T(8,128)(2,1)}, bf16[512,1024]{0,1:T(8,128)(2,1)S(1)}, u32[]{:S(2)}) copy-start(bf16[512,1024]{0,1:T(8,128)(2,1)S(1)} %copy.67) | copy-start | bytes 3145732
  38.0 27.7 %collective-permute-start.5 = (bf16[2,64,2304]{2,1,0:T(8,128)(2,1)S(1)}, bf16[2,64,2304]{2,1,0:T(8,128)(2,1)S(1)}, u32[]{:S(2)}, u32[]{:S(2)}) collective-permute-start(bf16[2,64,2304]{2,1,0:T(8,128)(2,1)S(1)} %maximum_bitcast_fusion), channel_id=1, source_target_pairs={{0,8},{2,10},{4,12},{6,14},{8,0},{10,2},{12,4},{14,6},{16,24},{18,... | collective-permute-start | bytes 1769480 | tf_op jit(solution)/shard_map/ppermute | solution.py:68
  42.6 26.6 %collective-permute-start = (bf16[512,1024]{0,1:T(8,128)(2,1)}, bf16[512,1024]{0,1:T(8,128)(2,1)}, u32[]{:S(2)}, u32[]{:S(2)}) collective-permute-start(bf16[512,1024]{0,1:T(8,128)(2,1)} %get-tuple-element.76), channel_id=1, source_target_pairs={{0,1},{1,0},{2,3},{3,2},{4,5},{5,4},{6,7},{7,6},{8,9},{9,8},{10,11... | collective-permute-start | bytes 3145736 | tf_op jit(solution)/shard_map/ppermute | solution.py:30
  65.8 29.1 %collective-permute-start.6 = (bf16[4,64,2304]{2,1,0:T(8,128)(2,1)S(1)}, bf16[4,64,2304]{2,1,0:T(8,128)(2,1)S(1)}, u32[]{:S(2)}, u32[]{:S(2)}) collective-permute-start(bf16[4,64,2304]{2,1,0:T(8,128)(2,1)S(1)} %bitcast.115), channel_id=1, source_target_pairs={{0,4},{2,6},{4,0},{6,2},{8,12},{10,14},{12,8},{14,10},{16,20},{18,... | collective-permute-start | bytes 3538952 | tf_op jit(solution)/shard_map/ppermute | solution.py:68
  67.4 53.4 %collective-permute-start.3 = (bf16[512,1024]{1,0:T(8,128)(2,1)}, bf16[512,1024]{1,0:T(8,128)(2,1)}, u32[]{:S(2)}, u32[]{:S(2)}) collective-permute-start(bf16[512,1024]{1,0:T(8,128)(2,1)} %param.10), channel_id=1, source_target_pairs={{0,1},{1,0},{2,3},{3,2},{4,5},{5,4},{6,7},{7,6},{8,9},{9,8},{10,11... | collective-permute-start | bytes 3145736 | tf_op jit(solution)/shard_map/ppermute | solution.py:30
  69.2 34.4 %copy-start.36 = (f32[1,512]{1,0:T(1,128)}, f32[1,512]{1,0:T(1,128)S(1)}, u32[]{:S(2)}) copy-start(f32[1,512]{1,0:T(1,128)S(1)} %get-tuple-element.93) | copy-start | bytes 6148
  69.2 34.4 %copy-start.38 = (f32[1,512]{1,0:T(1,128)}, f32[1,512]{1,0:T(1,128)S(1)}, u32[]{:S(2)}) copy-start(f32[1,512]{1,0:T(1,128)S(1)} %get-tuple-element.94) | copy-start | bytes 6148
  69.2 34.4 %copy-start.40 = (f32[1,512]{1,0:T(1,128)}, f32[1,512]{1,0:T(1,128)S(1)}, u32[]{:S(2)}) copy-start(f32[1,512]{1,0:T(1,128)S(1)} %get-tuple-element.95) | copy-start | bytes 6148
  97.0 50.2 %collective-permute-start.7 = (bf16[8,64,2304]{2,1,0:T(8,128)(2,1)}, bf16[8,64,2304]{2,1,0:T(8,128)(2,1)}, u32[]{:S(2)}, u32[]{:S(2)}) collective-permute-start(bf16[8,64,2304]{2,1,0:T(8,128)(2,1)} %bitcast.19), channel_id=1, source_target_pairs={{0,2},{2,0},{4,6},{6,4},{8,10},{10,8},{12,14},{14,12},{16,18},{18,... | collective-permute-start | bytes 7077896 | tf_op jit(solution)/shard_map/ppermute | solution.py:68
  114.3 25.9 %collective-permute-start.1 = (bf16[512,1024]{0,1:T(8,128)(2,1)}, bf16[512,1024]{0,1:T(8,128)(2,1)}, u32[]{:S(2)}, u32[]{:S(2)}) collective-permute-start(bf16[512,1024]{0,1:T(8,128)(2,1)} %dynamic-slice_convert_fusion.3), channel_id=1, source_target_pairs={{0,1},{1,0},{2,3},{3,2},{4,5},{5,4},{6,7},{7,6},{8,9},{9,8},{10,11... | collective-permute-start | bytes 3145736 | tf_op jit(solution)/shard_map/ppermute | solution.py:45
  145.7 24.7 %collective-permute-start.2 = (bf16[512,1024]{0,1:T(8,128)(2,1)S(1)}, bf16[512,1024]{0,1:T(8,128)(2,1)S(1)}, u32[]{:S(2)}, u32[]{:S(2)}) collective-permute-start(bf16[512,1024]{0,1:T(8,128)(2,1)S(1)} %get-tuple-element.70), channel_id=1, source_target_pairs={{0,1},{1,0},{2,3},{3,2},{4,5},{5,4},{6,7},{7,6},{8,9},{9,8},{10,11... | collective-permute-start | bytes 3145736 | tf_op jit(solution)/shard_map/ppermute | solution.py:30
  201.5 249.3 %reduce-scatter.5.cloned.1.call-start = ((), (), s32[]{:S(2)}) async-start(), calls=%async_computation.5 | async-start | bytes 10027008 | tf_op jit(solution)/shard_map/reduce_scatter | solution.py:152
  220.6 33.5 %slice-start.2 = ((s8[4718592]{0:T(1024)(128)(4,1)}), s8[524288]{0:T(1024)(128)(4,1)S(1)}, s32[]{:S(2)}) async-start(s8[4718592]{0:T(1024)(128)(4,1)} %bitcast.117), calls=%async_computation.8 | async-start | bytes 1048576
  252.6 35.5 %collective-permute-start.9 = (bf16[512,1024]{0,1:T(8,128)(2,1)}, bf16[512,1024]{0,1:T(8,128)(2,1)}, u32[]{:S(2)}, u32[]{:S(2)}) collective-permute-start(bf16[512,1024]{0,1:T(8,128)(2,1)} %dynamic-slice_convert_fusion.1), channel_id=1, source_target_pairs={{0,1},{1,0},{2,3},{3,2},{4,5},{5,4},{6,7},{7,6},{8,9},{9,8},{10,11... | collective-permute-start | bytes 3145736 | tf_op jit(solution)/shard_map/ppermute | solution.py:45
  263.6 35.6 %collective-permute-start.8 = (bf16[512,1024]{0,1:T(8,128)(2,1)}, bf16[512,1024]{0,1:T(8,128)(2,1)S(1)}, u32[]{:S(2)}, u32[]{:S(2)}) collective-permute-start(bf16[512,1024]{0,1:T(8,128)(2,1)} %dynamic-slice_convert_fusion.2), channel_id=1, source_target_pairs={{0,1},{1,0},{2,3},{3,2},{4,5},{5,4},{6,7},{7,6},{8,9},{9,8},{10,11... | collective-permute-start | bytes 3145736 | tf_op jit(solution)/shard_map/ppermute | solution.py:45
  311.7 22.9 %collective-permute-start.10 = (bf16[512,1024]{0,1:T(8,128)(2,1)S(1)}, bf16[512,1024]{0,1:T(8,128)(2,1)}, u32[]{:S(2)}, u32[]{:S(2)}) collective-permute-start(bf16[512,1024]{0,1:T(8,128)(2,1)S(1)} %get-tuple-element.67), channel_id=1, source_target_pairs={{0,1},{1,0},{2,3},{3,2},{4,5},{5,4},{6,7},{7,6},{8,9},{9,8},{10,11... | collective-permute-start | bytes 3145736 | tf_op jit(solution)/shard_map/ppermute | solution.py:30
  355.8 9.0 %collective-permute-start.12 = (bf16[8,64,2048]{2,1,0:T(8,128)(2,1)S(1)}, bf16[8,64,2048]{2,1,0:T(8,128)(2,1)}, u32[]{:S(2)}, u32[]{:S(2)}) collective-permute-start(bf16[8,64,2048]{2,1,0:T(8,128)(2,1)S(1)} %dynamic-slice_bitcast_fusion), channel_id=1, source_target_pairs={{0,2},{2,0},{4,6},{6,4},{8,10},{10,8},{12,14},{14,12},{16,18},{18,... | collective-permute-start | bytes 6291464 | tf_op jit(solution)/shard_map/ppermute | solution.py:89
  363.3 25.7 %collective-permute-start.11 = (bf16[512,1024]{0,1:T(8,128)(2,1)}, bf16[512,1024]{0,1:T(8,128)(2,1)}, u32[]{:S(2)}, u32[]{:S(2)}) collective-permute-start(bf16[512,1024]{0,1:T(8,128)(2,1)} %dynamic-slice_convert_fusion), channel_id=1, source_target_pairs={{0,1},{1,0},{2,3},{3,2},{4,5},{5,4},{6,7},{7,6},{8,9},{9,8},{10,11... | collective-permute-start | bytes 3145736 | tf_op jit(solution)/shard_map/ppermute | solution.py:45
  368.3 32.5 %collective-permute-start.13 = (bf16[4,64,2048]{2,1,0:T(8,128)(2,1)}, bf16[4,64,2048]{2,1,0:T(8,128)(2,1)}, u32[]{:S(2)}, u32[]{:S(2)}) collective-permute-start(bf16[4,64,2048]{2,1,0:T(8,128)(2,1)} %dynamic-slice_bitcast_fusion.1), channel_id=1, source_target_pairs={{0,4},{2,6},{4,0},{6,2},{8,12},{10,14},{12,8},{14,10},{16,20},{18,... | collective-permute-start | bytes 3145736 | tf_op jit(solution)/shard_map/ppermute | solution.py:89
  391.9 12.3 %collective-permute-start.16 = (f32[28,128]{1,0:T(8,128)S(1)}, f32[28,128]{1,0:T(8,128)S(1)}, u32[]{:S(2)}, u32[]{:S(2)}) collective-permute-start(f32[28,128]{1,0:T(8,128)S(1)} %maximum_bitcast_fusion.1), channel_id=1, source_target_pairs={{0,2},{2,0},{4,6},{6,4},{8,10},{10,8},{12,14},{14,12},{16,18},{18,... | collective-permute-start | bytes 43016 | tf_op jit(solution)/shard_map/ppermute | solution.py:55
  404.2 28.4 %collective-permute-start.14 = (bf16[2,64,2048]{2,1,0:T(8,128)(2,1)}, bf16[2,64,2048]{2,1,0:T(8,128)(2,1)}, u32[]{:S(2)}, u32[]{:S(2)}) collective-permute-start(bf16[2,64,2048]{2,1,0:T(8,128)(2,1)} %dynamic-slice_bitcast_fusion.2), channel_id=1, source_target_pairs={{0,8},{2,10},{4,12},{6,14},{8,0},{10,2},{12,4},{14,6},{16,24},{18,... | collective-permute-start | bytes 1572872 | tf_op jit(solution)/shard_map/ppermute | solution.py:89
  404.2 3.8 collective-permute-start.17
  408.0 10.3 %collective-permute-start.18 = (f32[28,128]{1,0:T(8,128)S(1)}, f32[28,128]{1,0:T(8,128)S(1)}, u32[]{:S(2)}, u32[]{:S(2)}) collective-permute-start(f32[28,128]{1,0:T(8,128)S(1)} %fusion.54), channel_id=1, source_target_pairs={{0,8},{2,10},{4,12},{6,14},{8,0},{10,2},{12,4},{14,6},{16,24},{18,... | collective-permute-start | bytes 43016 | tf_op jit(solution)/shard_map/ppermute | solution.py:55
  410.1 27.7 %copy-start.11 = (f32[512,1024]{0,1:T(8,128)S(1)}, f32[512,1024]{0,1:T(8,128)}, u32[]{:S(2)}) copy-start(f32[512,1024]{0,1:T(8,128)} %get-tuple-element.68) | copy-start | bytes 6291460
  410.1 27.7 %copy-start.42 = (f32[512]{0:T(512)S(1)}, f32[512]{0:T(512)}, u32[]{:S(2)}) copy-start(f32[512]{0:T(512)} %get-tuple-element.98) | copy-start | bytes 6148
  418.4 13.4 %collective-permute-start.19 = (f32[28,128]{1,0:T(8,128)S(1)}, f32[28,128]{1,0:T(8,128)S(1)}, u32[]{:S(2)}, u32[]{:S(2)}) collective-permute-start(f32[28,128]{1,0:T(8,128)S(1)} %add.212), channel_id=1, source_target_pairs={{0,16},{2,18},{4,20},{6,22},{8,24},{10,26},{12,28},{14,30},{16,0},... | collective-permute-start | bytes 43016 | tf_op jit(solution)/shard_map/ppermute | solution.py:55
  431.8 12.5 %collective-permute-start.20 = (f32[2,1024]{1,0:T(2,128)S(1)}, f32[2,1024]{1,0:T(2,128)S(1)}, u32[]{:S(2)}, u32[]{:S(2)}) collective-permute-start(f32[2,1024]{1,0:T(2,128)S(1)} %reshape.157), channel_id=1, source_target_pairs={{0,1},{1,0},{2,3},{3,2},{4,5},{5,4},{6,7},{7,6},{8,9},{9,8},{10,11... | collective-permute-start | bytes 24584 | tf_op jit(solution)/shard_map/ppermute | solution.py:55
  434.8 12.7 %collective-permute-start.15 = (bf16[1,64,2048]{2,1,0:T(8,128)(2,1)S(1)}, bf16[1,64,2048]{2,1,0:T(8,128)(2,1)}, u32[]{:S(2)}, u32[]{:S(2)}) collective-permute-start(bf16[1,64,2048]{2,1,0:T(8,128)(2,1)S(1)} %constant_dynamic-slice_fusion), channel_id=1, source_target_pairs={{0,16},{2,18},{4,20},{6,22},{8,24},{10,26},{12,28},{14,30},{16,0},... | collective-permute-start | bytes 786440 | tf_op jit(solution)/shard_map/ppermute | solution.py:89
  (44 other events, 315.9 us)
Sparse Core Ops, SparseCore 0:
  10.7 60.0 all-gather.2
  73.7 85.1 all-gather.4
  201.6 86.4 reduce-scatter.2
  292.1 115.7 reduce-scatter.4
